TPU v7x, 256 devices: a whole 4x4x8 slice. The times are simulated.
256 devices in a mesh: seq: 32 (over z, x), head: 8 (over y, core).
Axes of the slice: x: 4, y: 4, z: 8, core: 2. Of those that a mesh axis runs over, the one named last changes fastest.
Arguments:
- queries: bfloat16 [8192, 8192], P('seq', 'head'), may hold values from -6 to 6
- key_rows: bfloat16 [8192, 8192], P('seq', 'head'), may hold values from -6 to 6
- value_rows: bfloat16 [8192, 8192], P('seq', 'head'), may hold values from -160 to 160
- log_decay: float32 [8192, 64], P('seq', 'head'), may hold values from -0.5 to 0, as said below
- gate_input: bfloat16 [8192, 8192], P('seq', 'head'), may hold values from -12 to 12
- out_gain: float32 [8192], P('head'), may hold values from 0.1 to 1.9
- prior_state: float32 [64, 128, 128], P('head'), may hold values from -192 to 192
- out_grad: bfloat16 [8192, 8192], P('seq', 'head'), may hold values from -6 to 6
Outputs:
- attended: bfloat16 [8192, 8192], P('seq', 'head')
- grad_query: bfloat16 [8192, 8192], P('seq', 'head')
- grad_key: bfloat16 [8192, 8192], P('seq', 'head')
- grad_value: bfloat16 [8192, 8192], P('seq', 'head')
- grad_gate: bfloat16 [8192, 8192], P('seq', 'head')
Inputs may be any that keep to these rules, and one draw needn't show every extreme that they name: `log_decay`: every entry is negative; at each token a head's state is multiplied by exp(entry).
All inputs are finite; a program needn't handle non-finite values.
Results may differ from a plain program's by a relative error of at most 0.012.
Values sent between devices are 32-bit elements; how exact they have to be, the bound alone decides.
No kernel may reach another device: no remote copies, remote signals or barrier semaphores. Data moves between devices by JAX's collectives and lax.ppermute only.
A program may use at most 64 MiB of HBM per device.

v0:
```python
import jax
import jax.numpy as jnp
from jax import lax
from jax.sharding import PartitionSpec as P

BLK = 256
D = 8192


epsilon = 1e-06


def prefix(shard, axis, combine, identity, reverse):
    count, here = (lax.axis_size(axis), lax.axis_index(axis))
    everything = jax.tree.map(lambda part: lax.all_gather(part, axis), shard)
    start = jax.tree.map(
        lambda part, zero: jnp.broadcast_to(jnp.asarray(zero, part.dtype), part.shape),
        shard,
        identity,
    )

    def lap(k, before):
        at = count - 1 - k if reverse else k
        reached = at > here if reverse else at < here
        new = combine(before, jax.tree.map(lambda part: part[at], everything))
        return jax.tree.map(lambda a, b: jnp.where(reached, a, b), new, before)

    return lax.fori_loop(0, count, lap, start)


def decay_tables(decay_block):
    running = jnp.cumsum(decay_block, axis=0)
    closing = running[-1]
    spread = running.T[:, :, None] - running.T[:, None, :]
    causal = jnp.arange(decay_block.shape[0])[:, None] >= jnp.arange(decay_block.shape[0])[None, :]
    weights = jnp.where(causal[None], jnp.exp(jnp.minimum(spread, 0.0)), 0.0)
    return (running, closing, weights)


def split_parts(wide):
    upper = wide.astype(jnp.bfloat16)
    lower = (wide - upper.astype(jnp.float32)).astype(jnp.bfloat16)
    return (upper, lower)


def state_product(form, left, right):
    if left.dtype == jnp.float32:
        upper, lower = split_parts(left)
        return jnp.einsum(form, upper, right, preferred_element_type=jnp.float32) + jnp.einsum(
            form, lower, right, preferred_element_type=jnp.float32
        )
    upper, lower = split_parts(right)
    return jnp.einsum(form, left, upper, preferred_element_type=jnp.float32) + jnp.einsum(
        form, left, lower, preferred_element_type=jnp.float32
    )


def mixing_of(query_block, key_block, weights):
    scores = jnp.einsum("the,she->hts", query_block, key_block, preferred_element_type=jnp.float32)
    return (scores * weights).astype(jnp.bfloat16)


def chain_states(earlier, later):
    return (earlier[0] + later[0], jnp.exp(later[0])[:, None, None] * earlier[1] + later[1])


def local_forward(carried, inputs):
    query_block, key_block, value_block, decay_block = inputs
    running, closing, weights = decay_tables(decay_block)
    mixing = mixing_of(query_block, key_block, weights)
    within = jnp.einsum("hts,she->the", mixing, value_block, preferred_element_type=jnp.float32)
    across = jnp.exp(running)[:, :, None] * state_product("the,hef->thf", query_block, carried)
    remain = jnp.exp(closing[None, :] - running)
    updated = jnp.exp(closing)[:, None, None] * carried + state_product(
        "she,shf->hef", key_block.astype(jnp.float32) * remain[:, :, None], value_block
    )
    return (updated, (within + across, carried, mixing))


def backward_core(returned, inputs, tables, mixing):
    query_block, key_block, value_block, grad_rows, decay_block, opening = inputs[:6]
    running, closing, weights = tables
    grad_scores = jnp.einsum(
        "thf,shf->hts", grad_rows, value_block, preferred_element_type=jnp.float32
    )
    grad_mixing = (grad_scores * weights).astype(jnp.bfloat16)
    grad_q = jnp.einsum(
        "hts,she->the", grad_mixing, key_block, preferred_element_type=jnp.float32
    ) + jnp.exp(running)[:, :, None] * state_product("thf,hef->the", grad_rows, opening)
    remain = jnp.exp(closing[None, :] - running)[:, :, None]
    grad_k = jnp.einsum(
        "hts,the->she", grad_mixing, query_block, preferred_element_type=jnp.float32
    ) + remain * state_product("shf,hef->she", value_block, returned)
    grad_v = jnp.einsum(
        "hts,thf->shf", mixing, grad_rows, preferred_element_type=jnp.float32
    ) + remain * state_product("she,hef->shf", key_block, returned)
    summed = state_product(
        "the,thf->hef", query_block.astype(jnp.float32) * jnp.exp(running)[:, :, None], grad_rows
    )
    updated = summed + jnp.exp(closing)[:, None, None] * returned
    return (updated, (grad_q, grad_k, grad_v))


def shards(queries, key_rows, value_rows, log_decay, gate_input, out_gain, prior_state, out_grad):
    length, features = queries.shape
    head_count = log_decay.shape[1]
    head_size = features // head_count
    blocks = length // BLK
    block_shape = (blocks, BLK, head_count, head_size)
    token_shape = (length, head_count, head_size)
    query_all = queries.reshape(block_shape)
    key_all = key_rows.reshape(block_shape)
    value_all = value_rows.reshape(block_shape)
    decay_all = log_decay.reshape(blocks, BLK, head_count)
    zero_state = jnp.zeros((head_count, head_size, head_size), jnp.float32)
    zero_decay = jnp.zeros((head_count,), jnp.float32)
    local_state, (context_parts, openings, kept_mixing) = lax.scan(
        local_forward, zero_state, (query_all, key_all, value_all, decay_all)
    )
    through_dev = jnp.cumsum(log_decay, axis=0)
    decay_sum = through_dev[-1]
    prefix_decay, prefix_state = prefix(
        (decay_sum, local_state), "seq", chain_states, (zero_decay, zero_state), False
    )
    incoming = prefix_state + jnp.exp(prefix_decay)[:, None, None] * prior_state
    query_rows = queries.reshape(token_shape)
    context = context_parts.reshape(token_shape) + jnp.exp(through_dev)[:, :, None] * state_product(
        "the,hef->thf", query_rows, incoming
    )
    merged = context.reshape(length, features)
    squares = lax.psum(jnp.sum(merged * merged, axis=1), "head")
    inverse = lax.rsqrt(squares / D + epsilon)
    normed = merged * inverse[:, None]
    opened = jax.nn.sigmoid(gate_input.astype(jnp.float32))
    attended = (normed * out_gain * opened).astype(jnp.bfloat16)
    grad_wide = out_grad.astype(jnp.float32)
    grad_gate = (grad_wide * normed * out_gain * opened * (1.0 - opened)).astype(jnp.bfloat16)
    grad_norm = grad_wide * out_gain * opened
    row_dot = lax.psum(jnp.sum(merged * grad_norm, axis=1), "head")
    grad_merged = (
        inverse[:, None] * grad_norm - merged * (inverse * inverse * inverse * row_dot / D)[:, None]
    )
    grad_context = grad_merged.astype(jnp.bfloat16)
    grad_all = grad_context.reshape(block_shape)
    inputs_all = (query_all, key_all, value_all, grad_all, decay_all, openings)

    def backward_step(returned, inputs):
        return backward_core(returned, inputs, decay_tables(inputs[4]), inputs[6])

    local_returned, (grad_q_parts, grad_k_parts, grad_v_parts) = lax.scan(
        backward_step, zero_state, inputs_all + (kept_mixing,), reverse=True
    )
    grad_rows_all = grad_context.reshape(token_shape)
    grad_query = grad_q_parts.reshape(token_shape) + jnp.exp(through_dev)[
        :, :, None
    ] * state_product("thf,hef->the", grad_rows_all, incoming)
    suffix_decay, outgoing = prefix(
        (decay_sum, local_returned), "seq", chain_states, (zero_decay, zero_state), True
    )
    remain = jnp.exp(decay_sum[None, :] - through_dev)[:, :, None]
    value_tokens = value_rows.reshape(token_shape)
    key_tokens = key_rows.reshape(token_shape)
    grad_key = grad_k_parts.reshape(token_shape) + remain * state_product(
        "shf,hef->she", value_tokens, outgoing
    )
    grad_value = grad_v_parts.reshape(token_shape) + remain * state_product(
        "she,hef->shf", key_tokens, outgoing
    )
    return (
        attended,
        grad_query.reshape(length, features).astype(jnp.bfloat16),
        grad_key.reshape(length, features).astype(jnp.bfloat16),
        grad_value.reshape(length, features).astype(jnp.bfloat16),
        grad_gate,
    )


def solution(mesh):
    return jax.shard_map(
        shards,
        mesh=mesh,
        in_specs=(
            P("seq", "head"),
            P("seq", "head"),
            P("seq", "head"),
            P("seq", "head"),
            P("seq", "head"),
            P("head"),
            P("head", None, None),
            P("seq", "head"),
        ),
        out_specs=(
            P("seq", "head"),
            P("seq", "head"),
            P("seq", "head"),
            P("seq", "head"),
            P("seq", "head"),
        ),
        check_vma=False,
    )
```

profile of v0, /device:TPU:8, one launch (start us, length us, event | category | flops | bytes accessed | tf_op | source)
XLA Modules:
  0.0 406.1 jit_solution(2373041701965475646)
XLA Ops:
  7.2 1.3 reduce-window.14
  9.1 1.3 copy.126
  12.1 42.0 %all-gather.2 = f32[32,1,8]{2,1,0:T(1,128)S(1)} all-gather(f32[1,1,8]{2,1,0:T(1,128)S(1)} %bitcast.194), channel_id=1, replica_groups=mesh['seq'=32,'head'=8] {'seq'}, dimensions={0}, use_global_device_ids=true | all-gather | bytes 1056 | tf_op jit(solution)/shard_map/all_gather | solution.py:15
  56.4 98.2 %all-gather.6.cloned.1.call-done = f32[256,128,128]{2,1,0:T(8,128)} async-done(((f32[8,128,128]{2,1,0:T(8,128)}), f32[256,128,128]{2,1,0:T(8,128)}) %all-gather.6.cloned.1.call-update) | async-done | bytes 16777232 | tf_op jit(solution)/shard_map/all_gather | solution.py:15
  154.6 39.1 %while.21 = (s32[]{:T(128)}, f32[8]{0:T(128)S(1)}, f32[8,128,128]{2,1,0:T(8,128)S(1)}, s32[]{:T(128)}, f32[32,8]{1,0:T(8,128)S(1)}, /*index=5*/f32[32,8,128,128]{3,2,1,0:T(8,128)}, s32[]{:T(128)}, s32[]{:T(128)}) while((s32[]{:T(128)}, f32[8]{0:T(128)S(1)}, f32[8,128,128]{2,1,0:T(8,128)S(1)}, s32[]{:T(128)}, ...), condition=%wide.region_3.4_spmd.clone, body=%wide.region_2.3_spmd.clone.sunk | while | flops 524316 | bytes 1573147 | solution.py:28
  158.3 1.2 fusion.113
  159.5 1.2 fusion.113
  160.7 1.2 fusion.113
  161.9 1.2 fusion.113
  163.2 1.2 fusion.113
  164.4 1.2 fusion.113
  165.6 1.2 fusion.113
  166.8 1.2 fusion.113
  193.7 1.2 subtract_convert_fusion.6
  195.7 1.3 multiply_reduce_fusion.1
  197.0 1.6 copy.137
  198.6 1.5 multiply_reduce_fusion
  200.1 10.9 %all-reduce = (f32[256]{0:T(256)S(1)}, f32[256]{0:T(256)S(1)}) all-reduce(f32[256]{0:T(256)S(1)} %get-tuple-element.407, f32[256]{0:T(256)S(1)} %multiply_reduce_fusion), channel_id=1, replica_groups=mesh['seq'=32,'head'=8] {'head'}, use_global_device_ids=true, to_apply=%region_5.6 | all-reduce | flops 512 | bytes 4096 | tf_op jit(solution)/shard_map/psum | solution.py:131
  211.1 2.9 fusion.35
  219.5 2.6 convolution_bitcast_fusion.1
  222.4 130.6 %all-gather.8.cloned.1.call-done = f32[256,128,128]{2,1,0:T(8,128)} async-done(((f32[8,128,128]{2,1,0:T(8,128)}), f32[256,128,128]{2,1,0:T(8,128)}) %all-gather.8.cloned.1.call-update) | async-done | bytes 16777232 | tf_op jit(solution)/shard_map/all_gather | solution.py:15
  353.0 39.2 %while.22 = (s32[]{:T(128)}, f32[8,128,128]{2,1,0:T(8,128)S(1)}, s32[]{:T(128)}, f32[32,8]{1,0:T(8,128)S(1)}, f32[32,8,128,128]{3,2,1,0:T(8,128)}, /*index=5*/s32[]{:T(128)}, s32[]{:T(128)}, s32[]{:T(128)}, s32[]{:T(128)}) while((s32[]{:T(128)}, f32[8,128,128]{2,1,0:T(8,128)S(1)}, s32[]{:T(128)}, f32[32,8]{1,0:T(8,128)S(1)}, ...), condition=%wide.region_9.10_spmd.clone, body=%wide.region_8.9_spmd.clone.sunk | while | flops 524296 | bytes 1573135 | solution.py:28
  392.5 1.3 fusion.44
  396.4 1.5 fusion.21
  (181 shorter events, 82.1 us)
Async XLA Ops:
  7.2 3.2 copy-start
  7.2 147.4 %all-gather.6.cloned.1.call-start = ((), (), s32[]{:S(2)}) async-start(), calls=%async_computation | async-start | bytes 17301504 | tf_op jit(solution)/shard_map/all_gather | solution.py:15
  10.3 1.5 copy-start.8
  11.8 341.2 %all-gather.8.cloned.1.call-start = ((), (), s32[]{:S(2)}) async-start(), calls=%async_computation.1 | async-start | bytes 17301504 | tf_op jit(solution)/shard_map/all_gather | solution.py:15
  54.9 1.0 copy-start.2
  194.9 0.7 copy-start.5
  195.7 3.0 copy-start.9
  197.0 1.6 copy-start.7
  216.7 1.4 copy-start.3
  216.7 1.1 copy-start.6
  219.5 2.6 copy-start.4
  393.8 1.2 copy-start.1
Sparse Core Ops, SparseCore 0:
  11.9 142.6 all-gather.5
  215.8 137.2 all-gather.7
where the time goes:
time: 410 us; the launch traced here: 406 us
  waiting for transfers between devices  229 us (56%)
  other arithmetic  83.1 us (20%)
  blocking collectives  52.9 us (13%)
  matrix products  15.2 us (4%)
  between operations  14.3 us (3%)
  local copies, waits for them, and re-layouts  9.59 us (2%)
    all_gather x2, waiting for transfers between devices, prefix(): everything = jax.tree.map(lambda part: lax.all_gather(part, axis), shard)  229 us
    select_n x64, other arithmetic, lap(): return jax.tree.map(lambda a, b: jnp.where(reached, a, b), new, before)  75.2 us
    all_gather x1, blocking collectives, prefix(): everything = jax.tree.map(lambda part: lax.all_gather(part, axis), shard)  42 us
    psum x1, blocking collectives, shards(): squares = lax.psum(jnp.sum(merged * merged, axis=1), 'head')  10.9 us
  transfers between devices with their start and end apart: 2, of which 2 were waited for; matrix products, arithmetic and copies ran while one was open for 2% of the time, Pallas kernels for 0%

commit v1 on v0

v1 whole, which is shorter than its diff:
```python
import jax
import jax.numpy as jnp
from jax import lax
from jax.experimental import pallas as pl
from jax.experimental.pallas import tpu as pltpu
from jax.sharding import PartitionSpec as P

D = 8192
HD = 128
epsilon = 1e-06

F32 = jnp.float32
BF16 = jnp.bfloat16
MIB = 1 << 20


def dot(left, right, dims, precision=None):
    return lax.dot_general(
        left, right, (dims, ((), ())), precision=precision, preferred_element_type=F32
    )


NN = ((1,), (0,))
NT = ((1,), (1,))
TN = ((0,), (0,))


def cols(h):
    return slice(h * HD, (h + 1) * HD)


def exact_sum(table, decay):
    return dot(table.astype(F32), decay, NN, lax.Precision.HIGHEST)


def square_iota(n):
    row = lax.broadcasted_iota(jnp.int32, (n, n), 0)
    col = lax.broadcasted_iota(jnp.int32, (n, n), 1)
    return row, col


def state_kernel(k_ref, v_ref, decay_ref, out_ref, remain_ref):
    tokens, heads = decay_ref.shape
    row, col = square_iota(tokens)
    decay = decay_ref[...]
    remain = jnp.exp(exact_sum(col > row, decay))
    remain_ref[...] = remain
    closing = jnp.sum(decay, axis=0, keepdims=True)
    slices = out_ref.shape[0] // heads
    rows = HD // slices
    for h in range(heads):
        scaled = (v_ref[:, cols(h)].astype(F32) * remain[:, h : h + 1]).astype(BF16)
        state = dot(k_ref[:, cols(h)], scaled, TN)
        last = jnp.broadcast_to(closing[:, h : h + 1], (8, HD))
        for i in range(slices):
            out_ref[h * slices + i, 0:rows, :] = state[i * rows : (i + 1) * rows]
            out_ref[h * slices + i, rows : rows + 8, :] = last


def forward_chain_kernel(parts_ref, prior_ref, out_ref, factor_ref):
    count, rows, _ = out_ref.shape
    carried = prior_ref[0]
    for d in range(count):
        out_ref[d] = carried
        factor = jnp.exp(parts_ref[d, rows : rows + 8, :])
        factor_ref[d] = factor
        carried = factor[0:1] * carried + parts_ref[d, 0:rows, :]


def backward_chain_kernel(parts_ref, factor_ref, out_ref):
    count = out_ref.shape[0]
    returned = jnp.zeros(out_ref.shape[1:], F32)
    for d in range(count - 1, -1, -1):
        out_ref[d] = returned
        returned = factor_ref[d, 0:1, :] * returned + parts_ref[d]


def head_weights(running, running_rows, h, causal):
    spread = running[:, h : h + 1] - running_rows[h : h + 1, :]
    return jnp.where(causal, jnp.exp(jnp.minimum(spread, 0.0)), 0.0)


def within_kernel(
    q_ref, k_ref, v_ref, decay_ref, gate_ref, grad_ref, gain_ref,
    within_ref, mixing_ref, norm_grad_ref, grown_ref,
):
    tokens, heads = decay_ref.shape
    row, col = square_iota(tokens)
    causal = row >= col
    decay = decay_ref[...]
    running = exact_sum(causal, decay)
    running_rows = dot(decay, causal.astype(F32), ((0,), (1,)), lax.Precision.HIGHEST)
    grown_ref[...] = jnp.exp(running)
    for h in range(heads):
        c = cols(h)
        scores = dot(q_ref[:, c], k_ref[:, c], NT)
        mixing = (scores * head_weights(running, running_rows, h, causal)).astype(BF16)
        mixing_ref[h] = mixing
        within_ref[:, c] = dot(mixing, v_ref[:, c], NN)
        opened = jax.nn.sigmoid(gate_ref[:, c].astype(F32))
        norm_grad_ref[:, c] = grad_ref[:, c].astype(F32) * gain_ref[:, c] * opened


def context_kernel(
    q_ref, within_ref, norm_grad_ref, grown_ref, state_ref, context_ref, sums_ref
):
    tokens, heads = grown_ref.shape
    slices = state_ref.shape[0] // heads
    grown = grown_ref[...]
    squares = jnp.zeros((tokens, HD), F32)
    products = jnp.zeros((tokens, HD), F32)
    for h in range(heads):
        c = cols(h)
        state = state_ref[h * slices : (h + 1) * slices].reshape(HD, HD).astype(BF16)
        context = within_ref[:, c] + grown[:, h : h + 1] * dot(q_ref[:, c], state, NN)
        context_ref[:, c] = context
        squares += context * context
        products += context * norm_grad_ref[:, c]
    ones = jnp.ones((8, HD), F32)
    square_rows = dot(ones, squares, NT, lax.Precision.HIGHEST)
    product_rows = dot(ones, products, NT, lax.Precision.HIGHEST)
    first = lax.broadcasted_iota(jnp.int32, square_rows.shape, 0) == 0
    both = jnp.where(first, square_rows, product_rows)
    for p in range(sums_ref.shape[0]):
        sums_ref[p] = both


def gradient_kernel(
    sums_ref, q_ref, context_ref, norm_grad_ref, grown_ref, grad_ref, out_ref, inverse_ref
):
    tokens, heads = grown_ref.shape
    total = sums_ref[0]
    for p in range(1, sums_ref.shape[0]):
        total = total + sums_ref[p]
    pick = lax.broadcasted_iota(jnp.int32, (8, HD), 0)
    square = dot(total, (pick == 0).astype(F32), TN, lax.Precision.HIGHEST)
    product = dot(total, (pick == 1).astype(F32), TN, lax.Precision.HIGHEST)
    inverse = lax.rsqrt(square / D + epsilon)
    inverse_ref[...] = inverse
    slope = inverse * inverse * inverse * product / D
    grown = grown_ref[...]
    slices = out_ref.shape[0] // heads
    rows = HD // slices
    for h in range(heads):
        c = cols(h)
        grad = (inverse * norm_grad_ref[:, c] - context_ref[:, c] * slope).astype(BF16)
        grad_ref[:, c] = grad
        scaled = (q_ref[:, c].astype(F32) * grown[:, h : h + 1]).astype(BF16)
        state = dot(scaled, grad, TN)
        for i in range(slices):
            out_ref[h * slices + i] = state[i * rows : (i + 1) * rows]


def local_backward_kernel(
    q_ref, k_ref, v_ref, grad_ref, state_ref, mixing_ref, decay_ref, grown_ref,
    gate_ref, norm_grad_ref, context_ref, gain_ref, inverse_ref,
    attended_ref, grad_gate_ref, grad_q_ref, grad_k_ref, grad_v_ref,
):
    tokens, heads = decay_ref.shape
    row, col = square_iota(tokens)
    causal = row >= col
    decay = decay_ref[...]
    running = exact_sum(causal, decay)
    running_rows = dot(decay, causal.astype(F32), ((0,), (1,)), lax.Precision.HIGHEST)
    grown = grown_ref[...]
    inverse = inverse_ref[...]
    slices = state_ref.shape[0] // heads
    for h in range(heads):
        c = cols(h)
        opened = jax.nn.sigmoid(gate_ref[:, c].astype(F32))
        normed = context_ref[:, c] * inverse
        attended_ref[:, c] = (normed * gain_ref[:, c] * opened).astype(BF16)
        grad_gate_ref[:, c] = (norm_grad_ref[:, c] * normed * (1.0 - opened)).astype(BF16)
        grad = grad_ref[:, c]
        scores = dot(grad, v_ref[:, c], NT)
        weights = head_weights(running, running_rows, h, causal)
        grad_mixing = (scores * weights).astype(BF16)
        state = state_ref[h * slices : (h + 1) * slices].reshape(HD, HD).astype(BF16)
        across = grown[:, h : h + 1] * dot(grad, state, NT)
        grad_q_ref[:, c] = (dot(grad_mixing, k_ref[:, c], NN) + across).astype(BF16)
        grad_k_ref[:, c] = dot(grad_mixing, q_ref[:, c], TN)
        grad_v_ref[:, c] = dot(mixing_ref[h], grad, TN)


def finish_kernel(
    k_ref, v_ref, state_ref, remain_ref, part_k_ref, part_v_ref, grad_k_ref, grad_v_ref
):
    heads = remain_ref.shape[1]
    slices = state_ref.shape[0] // heads
    remain = remain_ref[...]
    for h in range(heads):
        c = cols(h)
        state = state_ref[h * slices : (h + 1) * slices].reshape(HD, HD).astype(BF16)
        keep = remain[:, h : h + 1]
        grad_k_ref[:, c] = (part_k_ref[:, c] + keep * dot(v_ref[:, c], state, NT)).astype(BF16)
        grad_v_ref[:, c] = (part_v_ref[:, c] + keep * dot(k_ref[:, c], state, NN)).astype(BF16)


def call(kernel, outs, *args, flops=0, limit=16):
    moved = sum(a.size * a.dtype.itemsize for a in args)
    moved += sum(s.size * s.dtype.itemsize for s in outs)
    vmem = pl.BlockSpec(memory_space=pltpu.VMEM)
    return pl.pallas_call(
        kernel,
        out_shape=tuple(outs),
        in_specs=[vmem] * len(args),
        out_specs=tuple([vmem] * len(outs)),
        compiler_params=pltpu.CompilerParams(vmem_limit_bytes=limit * MIB),
        cost_estimate=pl.CostEstimate(flops=flops, bytes_accessed=moved, transcendentals=0),
        name=kernel.__name__,
    )(*args)


def shape(dims, dtype=F32):
    return jax.ShapeDtypeStruct(dims, dtype)


def shards(queries, key_rows, value_rows, log_decay, gate_input, out_gain, prior_state, out_grad):
    tokens, features = queries.shape
    heads = log_decay.shape[1]
    count = lax.axis_size("seq")
    peers = lax.axis_size("head")
    rows = heads * HD // count
    piece = (count, rows, HD)
    wide = (tokens, features)
    gain = out_gain[None, :]
    product = 2 * tokens * HD * HD * heads

    parts, remain = call(
        state_kernel,
        [shape((count, rows + 8, HD)), shape((tokens, heads))],
        key_rows, value_rows, log_decay, flops=product,
    )
    parts = lax.all_to_all(parts, "seq", 0, 0)
    within, mixing, norm_grad, grown = call(
        within_kernel,
        [shape(wide), shape((heads, tokens, tokens), BF16), shape(wide), shape((tokens, heads))],
        queries, key_rows, value_rows, log_decay, gate_input, out_grad, gain,
        flops=4 * product, limit=24,
    )
    prior = lax.dynamic_index_in_dim(prior_state.reshape(piece), lax.axis_index("seq"), 0)
    opening, factor = call(
        forward_chain_kernel, [shape(piece), shape((count, 8, HD))], parts, prior
    )
    opening = lax.all_to_all(opening, "seq", 0, 0)
    context, sums = call(
        context_kernel,
        [shape(wide), shape((peers, 8, tokens))],
        queries, within, norm_grad, grown, opening, flops=product,
    )
    sums = lax.all_to_all(sums, "head", 0, 0)
    grad, parts, inverse = call(
        gradient_kernel,
        [shape(wide, BF16), shape(piece), shape((tokens, HD))],
        sums, queries, context, norm_grad, grown, flops=product,
    )
    parts = lax.all_to_all(parts, "seq", 0, 0)
    attended, grad_gate, grad_query, part_k, part_v = call(
        local_backward_kernel,
        [shape(wide, BF16), shape(wide, BF16), shape(wide, BF16), shape(wide), shape(wide)],
        queries, key_rows, value_rows, grad, opening, mixing, log_decay, grown,
        gate_input, norm_grad, context, gain, inverse,
        flops=9 * product, limit=24,
    )
    (returned,) = call(backward_chain_kernel, [shape(piece)], parts, factor)
    returned = lax.all_to_all(returned, "seq", 0, 0)
    grad_key, grad_value = call(
        finish_kernel,
        [shape(wide, BF16), shape(wide, BF16)],
        key_rows, value_rows, returned, remain, part_k, part_v, flops=2 * product,
    )
    return attended, grad_query, grad_key, grad_value, grad_gate


def solution(mesh):
    wide = P("seq", "head")
    return jax.shard_map(
        shards,
        mesh=mesh,
        in_specs=(wide, wide, wide, wide, wide, P("head"), P("head", None, None), wide),
        out_specs=(wide,) * 5,
        check_vma=False,
    )
```

time: 410 us -> 126 us (0.31)
  waiting for transfers between devices: 229 us -> 35.9 us
  other arithmetic: 83.1 us -> 0 us
  blocking collectives: 52.9 us -> 30.8 us
  starting transfers between devices: 0.08 us -> 21.5 us
  Pallas kernels: 0 us -> 15.8 us
  matrix products: 15.2 us -> 0 us
  between operations: 14.3 us -> 0.84 us
  local copies, waits for them, and re-layouts: 9.59 us -> 19.5 us
    all_gather x2 -> x0, waiting for transfers between devices: 229 us -> none  [prefix(): everything = jax.tree.map(lambda part: lax.all_gather(part, axis), shard)]
    select_n x64 -> x0, other arithmetic: 75.2 us -> none  [lap(): return jax.tree.map(lambda a, b: jnp.where(reached, a, b), new, before)]
    all_gather x1 -> x0, blocking collectives: 42 us -> none  [prefix(): everything = jax.tree.map(lambda part: lax.all_gather(part, axis), shard)]
    all_to_all x0 -> x3, waiting for transfers between devices: none -> 35.9 us  [the longest x1 20.2 us: shards(): parts = lax.all_to_all(parts, 'seq', 0, 0)]
    all_to_all x0 -> x2, blocking collectives: none -> 30.8 us  [the longest x1 21.9 us: shards(): parts = lax.all_to_all(parts, 'seq', 0, 0)]
    all_to_all x0 -> x3, starting transfers between devices: none -> 21.5 us  [the longest x1 11.3 us: shards(): parts = lax.all_to_all(parts, 'seq', 0, 0)]
    pallas_call x0 -> x8, Pallas kernels: none -> 15.8 us  [call(): pl.pallas_call(kernel, out_shape=tuple(outs), in_specs=[vmem] * len(args)...]
    dot_general x22 -> x0, matrix products: 15.2 us -> none  [the longest x8 4.55 us: state_product(): jnp.einsum(form, left, upper, preferred_element_type=jnp.float32)]
  transfers between devices with their start and end apart: 2 -> 3, of which waited for: 2 -> 3; matrix products, arithmetic and copies ran while one was open for 2% -> 0% of each run, Pallas kernels for 0% -> 6%
where the time goes in v1:
time: 126 us; the launch traced here: 124 us
  waiting for transfers between devices  35.9 us (28%)
  blocking collectives  30.8 us (24%)
  starting transfers between devices  21.5 us (17%)
  local copies, waits for them, and re-layouts  19.5 us (15%)
  Pallas kernels  15.8 us (13%)
    all_to_all x1, blocking collectives, shards(): parts = lax.all_to_all(parts, 'seq', 0, 0)  21.9 us
    all_to_all x1, waiting for transfers between devices, shards(): parts = lax.all_to_all(parts, 'seq', 0, 0)  20.2 us
    unnamed x55, local copies, waits for them, and re-layouts  19.5 us
    pallas_call x8, Pallas kernels, call(): pl.pallas_call(kernel, out_shape=tuple(outs), in_specs=[vmem] * len(args)...  15.8 us
    all_to_all x1, starting transfers between devices, shards(): parts = lax.all_to_all(parts, 'seq', 0, 0)  11.3 us
    all_to_all x1, waiting for transfers between devices, shards(): opening = lax.all_to_all(opening, 'seq', 0, 0)  11.1 us
    all_to_all x1, blocking collectives, shards(): sums = lax.all_to_all(sums, 'head', 0, 0)  8.9 us
    all_to_all x1, starting transfers between devices, shards(): opening = lax.all_to_all(opening, 'seq', 0, 0)  5.26 us
  transfers between devices with their start and end apart: 3, of which 3 were waited for; matrix products, arithmetic and copies ran while one was open for 0% of the time, Pallas kernels for 6%

profile of v1, /device:TPU:8, one launch (start us, length us, event | category | flops | bytes accessed | tf_op | source)
XLA Modules:
  0.0 124.4 jit_solution(7458812556833921674)
XLA Ops:
  1.5 1.0 copy-done.2
  2.6 1.0 copy-done.4
  3.6 1.8 %state_kernel.1 = (f32[32,40,128]{2,1,0:T(8,128)}, f32[256,8]{1,0:T(8,128)S(1)}) custom-call(bf16[256,1024]{1,0:T(8,128)(2,1)S(1)} %copy-done.2, bf16[256,1024]{1,0:T(8,128)(2,1)S(1)} %copy-done.4, f32[256,8]{1,0:T(8,128)S(1)} %copy.13.decay_ref), custom_call_target="tpu_custom_call" | custom-call | flops 67108864 | bytes 1720320 | tf_op jit(solution)/shard_map/state_kernel/pallas_call | solution.py:203
  6.1 11.3 %all-to-all-start = ((f32[32,40,128]{2,1,0:T(8,128)}), f32[32,40,128]{2,1,0:T(8,128)S(1)}, u32[]{:S(2)}, u32[]{:S(2)}) async-start(f32[32,40,128]{2,1,0:T(8,128)} %get-tuple-element.28), calls=%async_computation | async-start | bytes 1310720 | tf_op jit(solution)/shard_map/all_to_all | solution.py:234
  17.5 20.2 %all-to-all-done.parts_ref = f32[32,40,128]{2,1,0:T(8,128)S(1)} async-done(((f32[32,40,128]{2,1,0:T(8,128)}), f32[32,40,128]{2,1,0:T(8,128)S(1)}, u32[]{:S(2)}, u32[]{:S(2)}) %all-to-all-start) | async-done | bytes 655392 | tf_op jit(solution)/shard_map/all_to_all | solution.py:234
  38.5 5.3 %all-to-all-start.1 = ((f32[32,32,128]{2,1,0:T(8,128)}), f32[32,32,128]{2,1,0:T(8,128)}, u32[]{:S(2)}, u32[]{:S(2)}) async-start(f32[32,32,128]{2,1,0:T(8,128)} %get-tuple-element.29), calls=%async_computation.1 | async-start | bytes 1048576 | tf_op jit(solution)/shard_map/all_to_all | solution.py:245
  44.9 1.0 copy-done.21
  45.9 1.7 %within_kernel.1 = (f32[256,1024]{1,0:T(8,128)S(1)}, bf16[8,256,256]{2,1,0:T(8,128)(2,1)S(1)}, f32[256,1024]{1,0:T(8,128)S(1)}, f32[256,8]{1,0:T(8,128)S(1)}) custom-call(bf16[256,1024]{1,0:T(8,128)(2,1)S(1)} %copy-done.1, bf16[256,1024]{1,0:T(8,128)(2,1)S(1)} %copy-done.3, bf16[256,1024]{1,0:T(8,128)(2,1)S(1)} %copy-done.5, f32[256,8]{1,0:T(8,128)S(1)} %copy.13.decay_ref, ...), custom_call_target="tpu_custom_call" | custom-call | flops 268435456 | bytes 5787648 | tf_op jit(solution)/shard_map/within_kernel/pallas_call | solution.py:203
  49.5 11.1 %all-to-all-done.1.state_ref = f32[32,32,128]{2,1,0:T(8,128)} async-done(((f32[32,32,128]{2,1,0:T(8,128)}), f32[32,32,128]{2,1,0:T(8,128)}, u32[]{:S(2)}, u32[]{:S(2)}) %all-to-all-start.1) | async-done | bytes 524320 | tf_op jit(solution)/shard_map/all_to_all | solution.py:245
  60.6 1.2 copy-done.12
  61.9 1.8 %context_kernel.1 = (f32[256,1024]{1,0:T(8,128)S(1)}, f32[8,8,256]{2,1,0:T(8,128)S(1)}) custom-call(bf16[256,1024]{1,0:T(8,128)(2,1)S(1)} %copy-done.1, f32[256,1024]{1,0:T(8,128)S(1)} %copy-done.12, f32[256,1024]{1,0:T(8,128)S(1)} %get-tuple-element.26.norm_grad_ref, f32[256,8]{1,0:T(8,128)S(1)} %get-tuple-element.27.grown_ref, ...), custom_call_target="tpu_custom_call" | custom-call | flops 67108864 | bytes 4268032 | tf_op jit(solution)/shard_map/context_kernel/pallas_call | solution.py:203
  63.6 8.9 %all_to_all.25.sums_ref = f32[8,8,256]{2,1,0:T(8,128)S(1)} all-to-all(f32[8,8,256]{2,1,0:T(8,128)S(1)} %get-tuple-element.30), channel_id=1, replica_groups=mesh['seq'=32,'head'=8] {'head'}, dimensions={0} | all-to-all | bytes 131072 | tf_op jit(solution)/shard_map/all_to_all | solution.py:251
  72.5 1.2 gradient_kernel.1
  73.8 21.9 %all_to_all.26.parts_ref = f32[32,32,128]{2,1,0:T(8,128)S(1)} all-to-all(f32[32,32,128]{2,1,0:T(8,128)S(1)} %get-tuple-element.37), channel_id=1, replica_groups=mesh['seq'=32,'head'=8] {'seq'}, dimensions={0} | all-to-all | bytes 1048576 | tf_op jit(solution)/shard_map/all_to_all | solution.py:257
  96.6 5.0 %all-to-all-start.4 = ((f32[32,32,128]{2,1,0:T(8,128)}), f32[32,32,128]{2,1,0:T(8,128)}, u32[]{:S(2)}, u32[]{:S(2)}) async-start(f32[32,32,128]{2,1,0:T(8,128)} %copy-done.10), calls=%async_computation.4 | async-start | bytes 1048576 | tf_op jit(solution)/shard_map/all_to_all | solution.py:266
  101.6 1.2 copy-done.7
  102.8 1.0 copy-done.9
  103.9 1.2 copy-done.14
  105.1 1.0 copy-done.20
  106.1 5.8 %local_backward_kernel.1 = (bf16[256,1024]{1,0:T(8,128)(2,1)}, bf16[256,1024]{1,0:T(8,128)(2,1)}, bf16[256,1024]{1,0:T(8,128)(2,1)}, f32[256,1024]{1,0:T(8,128)S(1)}, f32[256,1024]{1,0:T(8,128)S(1)}) custom-call(bf16[256,1024]{1,0:T(8,128)(2,1)S(1)} %copy-done.1, bf16[256,1024]{1,0:T(8,128)(2,1)S(1)} %copy-done.3, bf16[256,1024]{1,0:T(8,128)(2,1)S(1)} %copy-done.5, ...), custom_call_target="tpu_custom_call" | custom-call | flops 603979776 | bytes 10113024 | tf_op jit(solution)/shard_map/local_backward_kernel/pallas_call | solution.py:203
  113.9 4.7 %all-to-all-done.4.state_ref = f32[32,32,128]{2,1,0:T(8,128)} async-done(((f32[32,32,128]{2,1,0:T(8,128)}), f32[32,32,128]{2,1,0:T(8,128)}, u32[]{:S(2)}, u32[]{:S(2)}) %all-to-all-start.4) | async-done | bytes 524320 | tf_op jit(solution)/shard_map/all_to_all | solution.py:266
  118.5 1.2 copy-done.16
  119.8 1.2 copy-done.18
  121.9 2.5 %finish_kernel.1 = (bf16[256,1024]{1,0:T(8,128)(2,1)}, bf16[256,1024]{1,0:T(8,128)(2,1)}) custom-call(bf16[256,1024]{1,0:T(8,128)(2,1)S(1)} %copy-done.3, bf16[256,1024]{1,0:T(8,128)(2,1)S(1)} %copy-done.5, f32[32,32,128]{2,1,0:T(8,128)} %all-to-all-done.4.state_ref, f32[256,8]{1,0:T(8,128)S(1)} %copy-done.25, f32[256,1024]{1,0:T(8,128)S(1)} %copy-done.16, ...), custom_call_target="tpu_custom_call" | custom-call | flops 134217728 | bytes 4726784 | tf_op jit(solution)/shard_map/finish_kernel/pallas_call | solution.py:203
  (48 shorter events, 9.2 us)
Async XLA Ops:
  0.6 16.8 %copy-start = (f32[8,128,128]{2,1,0:T(8,128)S(1)}, f32[8,128,128]{2,1,0:T(8,128)}, u32[]{:S(2)}) copy-start(f32[8,128,128]{2,1,0:T(8,128)} %param.14) | copy-start | bytes 1572868
  1.5 1.0 copy-start.2
  2.6 1.0 copy-start.4
  6.1 31.5 %all-to-all-start = ((f32[32,40,128]{2,1,0:T(8,128)}), f32[32,40,128]{2,1,0:T(8,128)S(1)}, u32[]{:S(2)}, u32[]{:S(2)}) async-start(f32[32,40,128]{2,1,0:T(8,128)} %get-tuple-element.28), calls=%async_computation | async-start | bytes 1310720 | tf_op jit(solution)/shard_map/all_to_all | solution.py:234
  37.6 6.2 %copy-start.5 = (bf16[256,1024]{1,0:T(8,128)(2,1)S(1)}, bf16[256,1024]{1,0:T(8,128)(2,1)}, u32[]{:S(2)}) copy-start(bf16[256,1024]{1,0:T(8,128)(2,1)} %v_ref.7) | copy-start | bytes 1572868
  37.6 6.2 %copy-start.26 = (f32[1024]{0:T(1024)S(1)}, f32[1024]{0:T(1024)}, u32[]{:S(2)}) copy-start(f32[1024]{0:T(1024)} %param.13) | copy-start | bytes 12292
  38.5 5.3 %copy-start.1 = (bf16[256,1024]{1,0:T(8,128)(2,1)S(1)}, bf16[256,1024]{1,0:T(8,128)(2,1)}, u32[]{:S(2)}) copy-start(bf16[256,1024]{1,0:T(8,128)(2,1)} %q_ref.7) | copy-start | bytes 1572868
  38.5 5.3 %copy-start.3 = (bf16[256,1024]{1,0:T(8,128)(2,1)S(1)}, bf16[256,1024]{1,0:T(8,128)(2,1)}, u32[]{:S(2)}) copy-start(bf16[256,1024]{1,0:T(8,128)(2,1)} %k_ref.7) | copy-start | bytes 1572868
  38.5 22.1 %all-to-all-start.1 = ((f32[32,32,128]{2,1,0:T(8,128)}), f32[32,32,128]{2,1,0:T(8,128)}, u32[]{:S(2)}, u32[]{:S(2)}) async-start(f32[32,32,128]{2,1,0:T(8,128)} %get-tuple-element.29), calls=%async_computation.1 | async-start | bytes 1048576 | tf_op jit(solution)/shard_map/all_to_all | solution.py:245
  43.8 1.0 copy-start.8
  44.9 1.0 copy-start.21
  60.6 1.2 copy-start.12
  63.6 10.1 %copy-start.6 = (f32[256,1024]{1,0:T(8,128)}, f32[256,1024]{1,0:T(8,128)S(1)}, u32[]{:S(2)}) copy-start(f32[256,1024]{1,0:T(8,128)S(1)} %get-tuple-element.31.context_ref) | copy-start | bytes 3145732
  73.8 22.0 %copy-start.19 = (bf16[256,1024]{1,0:T(8,128)(2,1)}, bf16[256,1024]{1,0:T(8,128)(2,1)S(1)}, u32[]{:S(2)}) copy-start(bf16[256,1024]{1,0:T(8,128)(2,1)S(1)} %get-tuple-element.32.grad_ref) | copy-start | bytes 1572868
  73.8 21.9 %copy-start.22 = (f32[256,128]{1,0:T(8,128)}, f32[256,128]{1,0:T(8,128)S(1)}, u32[]{:S(2)}) copy-start(f32[256,128]{1,0:T(8,128)S(1)} %get-tuple-element.34.inverse_ref) | copy-start | bytes 393220
  96.6 5.0 %copy-start.23 = (f32[256,128]{1,0:T(8,128)S(1)}, f32[256,128]{1,0:T(8,128)}, u32[]{:S(2)}) copy-start(f32[256,128]{1,0:T(8,128)} %copy-done.22) | copy-start | bytes 393220
  96.6 21.9 %all-to-all-start.4 = ((f32[32,32,128]{2,1,0:T(8,128)}), f32[32,32,128]{2,1,0:T(8,128)}, u32[]{:S(2)}, u32[]{:S(2)}) async-start(f32[32,32,128]{2,1,0:T(8,128)} %copy-done.10), calls=%async_computation.4 | async-start | bytes 1048576 | tf_op jit(solution)/shard_map/all_to_all | solution.py:266
  101.6 1.2 copy-start.7
  102.8 1.0 copy-start.9
  103.9 1.2 copy-start.14
  105.1 1.0 copy-start.20
  111.9 1.0 copy-start.15
  118.5 1.2 copy-start.16
  119.8 1.2 copy-start.18
  (6 other events, 5.3 us)

commit v2 on v1

v2 whole, which is shorter than its diff:
```python
import jax
import jax.numpy as jnp
from jax import lax
from jax.experimental import pallas as pl
from jax.experimental.pallas import tpu as pltpu
from jax.sharding import PartitionSpec as P

D = 8192
HD = 128
epsilon = 1e-06

F32 = jnp.float32
BF16 = jnp.bfloat16
MIB = 1 << 20


def dot(left, right, dims, precision=None):
    return lax.dot_general(
        left, right, (dims, ((), ())), precision=precision, preferred_element_type=F32
    )


NN = ((1,), (0,))
NT = ((1,), (1,))
TN = ((0,), (0,))


def cols(h):
    return slice(h * HD, (h + 1) * HD)


def token_sums(table, decay):
    return dot(table.astype(F32), decay, NT, lax.Precision.HIGHEST)


def square_iota(n):
    row = lax.broadcasted_iota(jnp.int32, (n, n), 0)
    col = lax.broadcasted_iota(jnp.int32, (n, n), 1)
    return row, col


def state_kernel(io, k_ref, v_ref, decay_ref, out_ref, remain_ref):
    heads, tokens = decay_ref.shape
    row, col = square_iota(tokens)
    decay = decay_ref[...]
    remain = jnp.exp(token_sums(col > row, decay))
    remain_ref[...] = remain
    closing = jnp.sum(decay, axis=1, keepdims=True)
    for h in range(heads):
        io.need(h)
        scaled = (v_ref[:, cols(h)].astype(F32) * remain[:, h : h + 1]).astype(BF16)
        out_ref[h, 0:HD, :] = dot(k_ref[:, cols(h)], scaled, TN)
        out_ref[h, HD : HD + 8, :] = jnp.broadcast_to(closing[h : h + 1], (8, HD))
        io.send(h)


def forward_total_kernel(io, parts_ref, total_ref, factor_ref):
    members = parts_ref.shape[0]
    carried = parts_ref[0, 0:HD, :]
    length = parts_ref[0, HD : HD + 8, :]
    factor_ref[0] = jnp.exp(length)
    for m in range(1, members):
        closing = parts_ref[m, HD : HD + 8, :]
        factor = jnp.exp(closing)
        factor_ref[m] = factor
        length = length + closing
        carried = factor[0:1] * carried + parts_ref[m, 0:HD, :]
    for g in range(total_ref.shape[0]):
        total_ref[g, 0:HD, :] = carried
        total_ref[g, HD : HD + 8, :] = length


def forward_chain_kernel(io, parts_ref, total_ref, factor_ref, prior_ref, out_ref, group_ref):
    members = parts_ref.shape[0]
    groups = total_ref.shape[0]
    here = lax.div(lax.axis_index("seq"), members)
    carried = prior_ref[0]
    for g in range(groups):
        factor = jnp.exp(total_ref[g, HD : HD + 8, :])
        group_ref[g] = factor
        if g < groups - 1:
            later = factor[0:1] * carried + total_ref[g, 0:HD, :]
            carried = jnp.where(g < here, later, carried)
    for m in range(members):
        out_ref[m] = carried
        if m < members - 1:
            carried = factor_ref[m, 0:1, :] * carried + parts_ref[m, 0:HD, :]


def backward_total_kernel(io, parts_ref, factor_ref, total_ref):
    members = parts_ref.shape[0]
    returned = parts_ref[members - 1]
    for m in range(members - 2, -1, -1):
        returned = factor_ref[m, 0:1, :] * returned + parts_ref[m]
    for g in range(total_ref.shape[0]):
        total_ref[g] = returned


def backward_chain_kernel(io, parts_ref, total_ref, factor_ref, group_ref, out_ref):
    members = parts_ref.shape[0]
    groups = total_ref.shape[0]
    here = lax.div(lax.axis_index("seq"), members)
    returned = jnp.zeros((HD, HD), F32)
    for g in range(groups - 1, 0, -1):
        earlier = group_ref[g, 0:1, :] * returned + total_ref[g]
        returned = jnp.where(g > here, earlier, returned)
    for m in range(members - 1, -1, -1):
        out_ref[m] = returned
        if m > 0:
            returned = factor_ref[m, 0:1, :] * returned + parts_ref[m]


def running_tables(decay, causal):
    rows = dot(decay, causal.astype(F32), NT, lax.Precision.HIGHEST)
    return token_sums(causal, decay), rows


def head_weights(running, running_rows, h, causal):
    spread = running[:, h : h + 1] - running_rows[h : h + 1, :]
    return jnp.where(causal, jnp.exp(jnp.minimum(spread, 0.0)), 0.0)


def within_kernel(
    io, q_ref, k_ref, v_ref, gate_ref, grad_ref, decay_ref, gain_ref,
    within_ref, norm_grad_ref, mixing_ref, grown_ref,
):
    heads, tokens = decay_ref.shape
    row, col = square_iota(tokens)
    causal = row >= col
    running, running_rows = running_tables(decay_ref[...], causal)
    grown_ref[...] = jnp.exp(running)
    for h in range(heads):
        io.need(h)
        c = cols(h)
        scores = dot(q_ref[:, c], k_ref[:, c], NT)
        mixing = (scores * head_weights(running, running_rows, h, causal)).astype(BF16)
        mixing_ref[h] = mixing
        within_ref[:, c] = dot(mixing, v_ref[:, c], NN)
        opened = jax.nn.sigmoid(gate_ref[:, c].astype(F32))
        norm_grad_ref[:, c] = grad_ref[:, c].astype(F32) * gain_ref[:, c] * opened
        io.send(h)


def context_kernel(
    io, q_ref, within_ref, norm_grad_ref, grown_ref, state_ref, context_ref, sums_ref
):
    tokens, heads = grown_ref.shape
    grown = grown_ref[...]
    squares = jnp.zeros((tokens, HD), F32)
    products = jnp.zeros((tokens, HD), F32)
    for h in range(heads):
        io.need(h)
        c = cols(h)
        across = dot(q_ref[:, c], state_ref[h].astype(BF16), NN)
        context = within_ref[:, c] + grown[:, h : h + 1] * across
        context_ref[:, c] = context
        squares += context * context
        products += context * norm_grad_ref[:, c]
    ones = jnp.ones((8, HD), F32)
    square_rows = dot(ones, squares, NT, lax.Precision.HIGHEST)
    product_rows = dot(ones, products, NT, lax.Precision.HIGHEST)
    first = lax.broadcasted_iota(jnp.int32, square_rows.shape, 0) == 0
    both = jnp.where(first, square_rows, product_rows)
    for p in range(sums_ref.shape[0]):
        sums_ref[p] = both


def gradient_kernel(
    io, q_ref, norm_grad_ref, sums_ref, context_ref, grown_ref, out_ref, grad_ref, inverse_ref
):
    tokens, heads = grown_ref.shape
    total = sums_ref[0]
    for p in range(1, sums_ref.shape[0]):
        total = total + sums_ref[p]
    pick = lax.broadcasted_iota(jnp.int32, (8, HD), 0)
    square = dot(total, (pick == 0).astype(F32), TN, lax.Precision.HIGHEST)
    product = dot(total, (pick == 1).astype(F32), TN, lax.Precision.HIGHEST)
    inverse = lax.rsqrt(square / D + epsilon)
    inverse_ref[...] = inverse
    slope = inverse * inverse * inverse * product / D
    grown = grown_ref[...]
    for h in range(heads):
        io.need(h)
        c = cols(h)
        grad = (inverse * norm_grad_ref[:, c] - context_ref[:, c] * slope).astype(BF16)
        grad_ref[:, c] = grad
        scaled = (q_ref[:, c].astype(F32) * grown[:, h : h + 1]).astype(BF16)
        out_ref[h] = dot(scaled, grad, TN)
        io.send(h)


def gate_kernel(
    io, gate_ref, norm_grad_ref, context_ref, gain_ref, inverse_ref, attended_ref, grad_gate_ref
):
    heads = context_ref.shape[1] // HD
    inverse = inverse_ref[...]
    for h in range(heads):
        io.need(h)
        c = cols(h)
        opened = jax.nn.sigmoid(gate_ref[:, c].astype(F32))
        normed = context_ref[:, c] * inverse
        attended_ref[:, c] = (normed * gain_ref[:, c] * opened).astype(BF16)
        grad_gate_ref[:, c] = (norm_grad_ref[:, c] * normed * (1.0 - opened)).astype(BF16)
        io.send(h)


def local_backward_kernel(
    io, q_ref, k_ref, v_ref, grad_ref, mixing_ref, state_ref, decay_ref, grown_ref,
    grad_q_ref, grad_k_ref, grad_v_ref,
):
    heads, tokens = decay_ref.shape
    row, col = square_iota(tokens)
    causal = row >= col
    running, running_rows = running_tables(decay_ref[...], causal)
    grown = grown_ref[...]
    for h in range(heads):
        io.need(h)
        c = cols(h)
        grad = grad_ref[:, c]
        scores = dot(grad, v_ref[:, c], NT)
        weights = head_weights(running, running_rows, h, causal)
        grad_mixing = (scores * weights).astype(BF16)
        across = grown[:, h : h + 1] * dot(grad, state_ref[h].astype(BF16), NT)
        grad_q_ref[:, c] = (dot(grad_mixing, k_ref[:, c], NN) + across).astype(BF16)
        grad_k_ref[:, c] = dot(grad_mixing, q_ref[:, c], TN)
        grad_v_ref[:, c] = dot(mixing_ref[h], grad, TN)
        io.send(h)


def finish_kernel(
    io, k_ref, v_ref, part_k_ref, part_v_ref, state_ref, remain_ref, grad_k_ref, grad_v_ref
):
    heads = remain_ref.shape[1]
    remain = remain_ref[...]
    for h in range(heads):
        io.need(h)
        c = cols(h)
        state = state_ref[h].astype(BF16)
        keep = remain[:, h : h + 1]
        grad_k_ref[:, c] = (part_k_ref[:, c] + keep * dot(v_ref[:, c], state, NT)).astype(BF16)
        grad_v_ref[:, c] = (part_v_ref[:, c] + keep * dot(k_ref[:, c], state, NN)).astype(BF16)
        io.send(h)


PAIR = 2


class Stream:
    def __init__(self, chunks, arrivals, departures):
        self.chunks, self.arrivals, self.departures = chunks, arrivals, departures
        for i in range(chunks):
            for copy in arrivals:
                copy(i).start()

    def need(self, h):
        if h % PAIR == 0:
            for copy in self.arrivals:
                copy(h // PAIR).wait()

    def send(self, h):
        if h % PAIR == PAIR - 1:
            for copy in self.departures:
                copy(h // PAIR).start()

    def finish(self):
        for i in range(self.chunks):
            for copy in self.departures:
                copy(i).wait()


def chunk_of(ref, i):
    if len(ref.shape) == 3:
        return ref.at[pl.ds(i * PAIR, PAIR)]
    return ref.at[:, pl.ds(i * PAIR * HD, PAIR * HD)]


def copier(source, target, sem, n):
    return lambda i: pltpu.make_async_copy(chunk_of(source, i), chunk_of(target, i), sem.at[n, i])


def call(kernel, outs, *args, stream_in=0, stream_out=0, chunks=1, flops=0, limit=16):
    moved = sum(a.size * a.dtype.itemsize for a in args)
    moved += sum(s.size * s.dtype.itemsize for s in outs)
    inside = pl.BlockSpec(memory_space=pltpu.VMEM)
    outside = pl.BlockSpec(memory_space=pltpu.HBM)
    n, m = len(args), len(outs)

    def body(*refs):
        ins, results, scratch = list(refs[:n]), list(refs[n : n + m]), refs[n + m :]
        arrivals, departures = [], []
        for j in range(stream_in):
            arrivals.append(copier(ins[j], scratch[j], scratch[-2], j))
            ins[j] = scratch[j]
        for j in range(stream_out):
            local = scratch[stream_in + j]
            departures.append(copier(local, results[j], scratch[-1], j))
            results[j] = local
        io = Stream(chunks, arrivals, departures)
        kernel(io, *ins, *results)
        io.finish()

    streamed = list(args[:stream_in]) + list(outs[:stream_out])
    args = [
        pltpu.with_memory_space_constraint(a, pltpu.HBM) if j < stream_in else a
        for j, a in enumerate(args)
    ]
    shapes = [pltpu.HBM(s.shape, s.dtype) if j < stream_out else s for j, s in enumerate(outs)]
    return pl.pallas_call(
        body,
        out_shape=tuple(shapes),
        in_specs=[outside] * stream_in + [inside] * (n - stream_in),
        out_specs=tuple([outside] * stream_out + [inside] * (m - stream_out)),
        scratch_shapes=[pltpu.VMEM(s.shape, s.dtype) for s in streamed]
        + [
            pltpu.SemaphoreType.DMA((max(stream_in, 1), chunks)),
            pltpu.SemaphoreType.DMA((max(stream_out, 1), chunks)),
        ],
        compiler_params=pltpu.CompilerParams(vmem_limit_bytes=limit * MIB),
        cost_estimate=pl.CostEstimate(flops=flops, bytes_accessed=moved, transcendentals=0),
        name=kernel.__name__,
    )(*args)


def shape(dims, dtype=F32):
    return jax.ShapeDtypeStruct(dims, dtype)


def shards(queries, key_rows, value_rows, log_decay, gate_input, out_gain, prior_state, out_grad):
    tokens, features = queries.shape
    heads = log_decay.shape[1]
    count = lax.axis_size("seq")
    peers = lax.axis_size("head")
    groups = count // heads
    near = [[g * heads + m for m in range(heads)] for g in range(groups)]
    far = [[g * heads + m for g in range(groups)] for m in range(heads)]
    wide = (tokens, features)
    states = (heads, HD, HD)
    gain = out_gain[None, :]
    decay = log_decay.T
    product = 2 * tokens * HD * HD * heads
    chunks = heads // PAIR

    def exchange(value, axis, members=None):
        return lax.all_to_all(value, axis, 0, 0, axis_index_groups=members)

    parts, remain = call(
        state_kernel,
        [shape((heads, HD + 8, HD)), shape((tokens, heads))],
        key_rows, value_rows, decay, stream_in=2, chunks=chunks, flops=product,
    )
    parts = exchange(parts, "seq", near)
    total, factor = call(
        forward_total_kernel, [shape((groups, HD + 8, HD)), shape((heads, 8, HD))], parts
    )
    total = exchange(total, "seq", far)
    within, norm_grad, mixing, grown = call(
        within_kernel,
        [shape(wide), shape(wide), shape((heads, tokens, tokens), BF16), shape((tokens, heads))],
        queries, key_rows, value_rows, gate_input, out_grad, decay, gain,
        stream_in=5, stream_out=3, chunks=chunks, flops=4 * product, limit=24,
    )
    place = lax.rem(lax.axis_index("seq"), heads)
    prior = lax.dynamic_index_in_dim(prior_state, place, 0)
    opening, group_factor = call(
        forward_chain_kernel,
        [shape(states), shape((groups, 8, HD))],
        parts, total, factor, prior,
    )
    opening = exchange(opening, "seq", near)
    context, sums = call(
        context_kernel,
        [shape(wide), shape((peers, 8, tokens))],
        queries, within, norm_grad, grown, opening,
        stream_in=3, chunks=chunks, flops=product,
    )
    sums = exchange(sums, "head")
    parts, grad, inverse = call(
        gradient_kernel,
        [shape(states), shape(wide, BF16), shape((tokens, HD))],
        queries, norm_grad, sums, context, grown,
        stream_in=2, chunks=chunks, flops=product,
    )
    parts = exchange(parts, "seq", near)
    attended, grad_gate = call(
        gate_kernel,
        [shape(wide, BF16), shape(wide, BF16)],
        gate_input, norm_grad, context, gain, inverse,
        stream_in=3, stream_out=2, chunks=chunks, flops=product,
    )
    grad_query, part_k, part_v = call(
        local_backward_kernel,
        [shape(wide, BF16), shape(wide), shape(wide)],
        queries, key_rows, value_rows, grad, mixing, opening, decay, grown,
        stream_in=6, stream_out=3, chunks=chunks, flops=9 * product, limit=24,
    )
    (total,) = call(backward_total_kernel, [shape((groups, HD, HD))], parts, factor)
    total = exchange(total, "seq", far)
    (returned,) = call(
        backward_chain_kernel, [shape(states)], parts, total, factor, group_factor
    )
    returned = exchange(returned, "seq", near)
    grad_key, grad_value = call(
        finish_kernel,
        [shape(wide, BF16), shape(wide, BF16)],
        key_rows, value_rows, part_k, part_v, returned, remain,
        stream_in=4, stream_out=2, chunks=chunks, flops=2 * product,
    )
    return attended, grad_query, grad_key, grad_value, grad_gate


def solution(mesh):
    wide = P("seq", "head")
    return jax.shard_map(
        shards,
        mesh=mesh,
        in_specs=(wide, wide, wide, wide, wide, P("head"), P("head", None, None), wide),
        out_specs=(wide,) * 5,
        check_vma=False,
    )
```

time: 126 us -> 109 us (0.87)
  waiting for transfers between devices: 35.9 us -> 13.8 us
  blocking collectives: 30.8 us -> 50.3 us
  local copies, waits for them, and re-layouts: 19.5 us -> 1.57 us
  Pallas kernels: 15.8 us -> 26 us
  starting transfers between devices: 21.5 us -> 14.6 us
    all_to_all x3, waiting for transfers between devices: 35.9 us -> 13.8 us  [exchange(): return lax.all_to_all(value, axis, 0, 0, axis_index_groups=members)]
    all_to_all x2 -> x4, blocking collectives: 30.8 us -> 50.3 us  [exchange(): return lax.all_to_all(value, axis, 0, 0, axis_index_groups=members)]
    unnamed x55 -> x14, local copies, waits for them, and re-layouts: 19.5 us -> 1.57 us
    pallas_call x8 -> x11, Pallas kernels: 15.8 us -> 26 us  [call(): pl.pallas_call(body, out_shape=tuple(shapes), in_specs=[outside] * stream...]
    all_to_all x3, starting transfers between devices: 21.5 us -> 14.6 us  [exchange(): return lax.all_to_all(value, axis, 0, 0, axis_index_groups=members)]
  transfers between devices with their start and end apart: 3 -> 3, of which waited for: 3 -> 2; matrix products, arithmetic and copies ran while one was open for 0% -> 0% of each run, Pallas kernels for 6% -> 12%
where the time goes in v2:
time: 109 us; the launch traced here: 107 us
  blocking collectives  50.3 us (46%)
  Pallas kernels  26 us (24%)
  starting transfers between devices  14.6 us (13%)
  waiting for transfers between devices  13.8 us (13%)
  local copies, waits for them, and re-layouts  1.57 us (1%)
    all_to_all x4, blocking collectives, exchange(): return lax.all_to_all(value, axis, 0, 0, axis_index_groups=members)  50.3 us
    pallas_call x11, Pallas kernels, call(): pl.pallas_call(body, out_shape=tuple(shapes), in_specs=[outside] * stream...  26 us
    all_to_all x3, starting transfers between devices, exchange(): return lax.all_to_all(value, axis, 0, 0, axis_index_groups=members)  14.6 us
    all_to_all x3, waiting for transfers between devices, exchange(): return lax.all_to_all(value, axis, 0, 0, axis_index_groups=members)  13.8 us
  transfers between devices with their start and end apart: 3, of which 2 were waited for; matrix products, arithmetic and copies ran while one was open for 0% of the time, Pallas kernels for 12%

profile of v2, /device:TPU:8, one launch (start us, length us, event | category | flops | bytes accessed | tf_op | source)
XLA Modules:
  0.0 107.1 jit_solution(15687966688136912000)
XLA Ops:
  0.6 0.0 copy-start
  0.6 0.0 copy-start.4
  0.7 0.7 copy-done.4
  1.4 2.6 %state_kernel.1 = (f32[8,136,128]{2,1,0:T(8,128)S(1)}, f32[256,8]{1,0:T(8,128)S(1)}) custom-call(bf16[256,1024]{1,0:T(8,128)(2,1)} %refs_0_.13, bf16[256,1024]{1,0:T(8,128)(2,1)} %refs_1_.7, f32[8,256]{1,0:T(8,128)S(1)} %bitcast.2), custom_call_target="tpu_custom_call" | custom-call | flops 67108864 | bytes 1622016 | tf_op jit(solution)/shard_map/state_kernel/pallas_call | solution.py:308
  4.0 16.1 %all_to_all.35.refs_0_ = f32[8,136,128]{2,1,0:T(8,128)S(1)} all-to-all(f32[8,136,128]{2,1,0:T(8,128)S(1)} %get-tuple-element.30), channel_id=1, replica_groups={{0,8,16,24,32,40,48,56},{64,72,80,88,96,104,112,120},{128,136,144,152,1..., dimensions={0} | all-to-all | bytes 1114112 | tf_op jit(solution)/shard_map/all_to_all | solution.py:344
  20.1 0.8 forward_total_kernel.1
  20.9 7.6 %all-to-all-start.1 = ((f32[4,136,128]{2,1,0:T(8,128)}), f32[4,136,128]{2,1,0:T(8,128)S(1)}, u32[]{:S(2)}, u32[]{:S(2)}) async-start(f32[4,136,128]{2,1,0:T(8,128)} %get-tuple-element.31), calls=%async_computation.1 | async-start | bytes 557056 | tf_op jit(solution)/shard_map/all_to_all | solution.py:344
  28.5 9.8 %all-to-all-done.1.refs_1_ = f32[4,136,128]{2,1,0:T(8,128)S(1)} async-done(((f32[4,136,128]{2,1,0:T(8,128)}), f32[4,136,128]{2,1,0:T(8,128)S(1)}, u32[]{:S(2)}, u32[]{:S(2)}) %all-to-all-start.1) | async-done | bytes 278560 | tf_op jit(solution)/shard_map/all_to_all | solution.py:344
  38.3 0.9 forward_chain_kernel.1
  39.2 3.5 %all-to-all-start.2 = ((f32[8,128,128]{2,1,0:T(8,128)}), f32[8,128,128]{2,1,0:T(8,128)S(1)}, u32[]{:S(2)}, u32[]{:S(2)}) async-start(f32[8,128,128]{2,1,0:T(8,128)} %get-tuple-element.33), calls=%async_computation.2 | async-start | bytes 1048576 | tf_op jit(solution)/shard_map/all_to_all | solution.py:344
  42.8 4.2 %within_kernel.1 = (f32[256,1024]{1,0:T(8,128)}, f32[256,1024]{1,0:T(8,128)}, bf16[8,256,256]{2,1,0:T(8,128)(2,1)}, f32[256,8]{1,0:T(8,128)S(1)}) custom-call(bf16[256,1024]{1,0:T(8,128)(2,1)} %refs_0_.12, bf16[256,1024]{1,0:T(8,128)(2,1)} %refs_0_.13, bf16[256,1024]{1,0:T(8,128)(2,1)} %refs_1_.7, bf16[256,1024]{1,0:T(8,128)(2,1)} %refs_0_.11, ...), custom_call_target="tpu_custom_call" | custom-call | flops 268435456 | bytes 5787648 | tf_op jit(solution)/shard_map/within_kernel/pallas_call | solution.py:308
  47.0 4.0 %all-to-all-done.2.refs_4_.refs_5_ = f32[8,128,128]{2,1,0:T(8,128)S(1)} async-done(((f32[8,128,128]{2,1,0:T(8,128)}), f32[8,128,128]{2,1,0:T(8,128)S(1)}, u32[]{:S(2)}, u32[]{:S(2)}) %all-to-all-start.2) | async-done | bytes 524320 | tf_op jit(solution)/shard_map/all_to_all | solution.py:344
  51.0 2.6 %context_kernel.1 = (f32[256,1024]{1,0:T(8,128)S(1)}, f32[8,8,256]{2,1,0:T(8,128)S(1)}) custom-call(bf16[256,1024]{1,0:T(8,128)(2,1)} %refs_0_.12, f32[256,1024]{1,0:T(8,128)} %get-tuple-element.28.refs_1_, f32[256,1024]{1,0:T(8,128)} %get-tuple-element.27.refs_2_.refs_1_, f32[256,8]{1,0:T(8,128)S(1)} %get-tuple-element.29.refs_3_.refs_4_.refs_7_, ...), custom_call_target="tpu_custom_call" | custom-call | flops 67108864 | bytes 4268032 | tf_op jit(solution)/shard_map/context_kernel/pallas_call | solution.py:308
  53.6 8.9 %all_to_all.36.refs_2_ = f32[8,8,256]{2,1,0:T(8,128)S(1)} all-to-all(f32[8,8,256]{2,1,0:T(8,128)S(1)} %get-tuple-element.35), channel_id=1, replica_groups=mesh['seq'=32,'head'=8] {'head'}, dimensions={0} | all-to-all | bytes 131072 | tf_op jit(solution)/shard_map/all_to_all | solution.py:344
  62.4 2.7 %gradient_kernel.1 = (f32[8,128,128]{2,1,0:T(8,128)S(1)}, bf16[256,1024]{1,0:T(8,128)(2,1)S(1)}, f32[256,128]{1,0:T(8,128)S(1)}) custom-call(bf16[256,1024]{1,0:T(8,128)(2,1)} %refs_0_.12, f32[256,1024]{1,0:T(8,128)} %get-tuple-element.27.refs_2_.refs_1_, f32[8,8,256]{2,1,0:T(8,128)S(1)} %all_to_all.36.refs_2_, ...), custom_call_target="tpu_custom_call" | custom-call | flops 67108864 | bytes 3874816 | tf_op jit(solution)/shard_map/gradient_kernel/pallas_call | solution.py:308
  65.2 0.8 copy-done.3
  66.0 12.9 %all_to_all.37.refs_0_ = f32[8,128,128]{2,1,0:T(8,128)S(1)} all-to-all(f32[8,128,128]{2,1,0:T(8,128)S(1)} %get-tuple-element.43), channel_id=1, replica_groups={{0,8,16,24,32,40,48,56},{64,72,80,88,96,104,112,120},{128,136,144,152,1..., dimensions={0} | all-to-all | bytes 1048576 | tf_op jit(solution)/shard_map/all_to_all | solution.py:344
  78.8 0.1 backward_total_kernel.1
  78.9 12.5 %all_to_all.38.refs_1_ = f32[4,128,128]{2,1,0:T(8,128)S(1)} all-to-all(f32[4,128,128]{2,1,0:T(8,128)S(1)} %backward_total_kernel.1), channel_id=1, replica_groups={{0,64,128,192},{8,72,136,200},{16,80,144,208},{24,88,152,216},{32,96,16..., dimensions={0} | all-to-all | bytes 524288 | tf_op jit(solution)/shard_map/all_to_all | solution.py:344
  91.4 0.9 backward_chain_kernel.1
  92.2 3.5 %all-to-all-start.6 = ((f32[8,128,128]{2,1,0:T(8,128)}), f32[8,128,128]{2,1,0:T(8,128)S(1)}, u32[]{:S(2)}, u32[]{:S(2)}) async-start(f32[8,128,128]{2,1,0:T(8,128)} %backward_chain_kernel.1), calls=%async_computation.6 | async-start | bytes 1048576 | tf_op jit(solution)/shard_map/all_to_all | solution.py:344
  95.7 2.7 %gate_kernel.1 = (bf16[256,1024]{1,0:T(8,128)(2,1)}, bf16[256,1024]{1,0:T(8,128)(2,1)}) custom-call(bf16[256,1024]{1,0:T(8,128)(2,1)} %refs_0_.11, f32[256,1024]{1,0:T(8,128)} %get-tuple-element.27.refs_2_.refs_1_, f32[256,1024]{1,0:T(8,128)} %copy-done.2, f32[1,1024]{1,0:T(1,128)S(1)} %bitcast.6, f32[256,128]{1,0:T(8,128)S(1)} %get-tuple-element.36.refs_4_), custom_call_target="tpu_custom_call" | custom-call | flops 67108864 | bytes 3805184 | tf_op jit(solution)/shard_map/gate_kernel/pallas_call | solution.py:308
  98.4 5.6 %local_backward_kernel.1 = (bf16[256,1024]{1,0:T(8,128)(2,1)}, f32[256,1024]{1,0:T(8,128)}, f32[256,1024]{1,0:T(8,128)}) custom-call(bf16[256,1024]{1,0:T(8,128)(2,1)} %refs_0_.12, bf16[256,1024]{1,0:T(8,128)(2,1)} %refs_0_.13, bf16[256,1024]{1,0:T(8,128)(2,1)} %refs_1_.7, bf16[256,1024]{1,0:T(8,128)(2,1)} %copy-done.3, ...), custom_call_target="tpu_custom_call" | custom-call | flops 603979776 | bytes 6307840 | tf_op jit(solution)/shard_map/local_backward_kernel/pallas_call | solution.py:308
  104.1 3.1 %finish_kernel.1 = (bf16[256,1024]{1,0:T(8,128)(2,1)}, bf16[256,1024]{1,0:T(8,128)(2,1)}) custom-call(bf16[256,1024]{1,0:T(8,128)(2,1)} %refs_0_.13, bf16[256,1024]{1,0:T(8,128)(2,1)} %refs_1_.7, f32[256,1024]{1,0:T(8,128)} %get-tuple-element.41.refs_2_, f32[256,1024]{1,0:T(8,128)} %get-tuple-element.42.refs_3_, f32[8,128,128]{2,1,0:T(8,128)S(1)} %all-to-all-done.6.refs_4_, ...), custom_call_target="tpu_custom_call" | custom-call | flops 134217728 | bytes 4726784 | tf_op jit(solution)/shard_map/finish_kernel/pallas_call | solution.py:308
  (12 shorter events, 0.0 us)
Async XLA Ops:
  0.6 27.9 %copy-start = (f32[8,128,128]{2,1,0:T(8,128)S(1)}, f32[8,128,128]{2,1,0:T(8,128)}, u32[]{:S(2)}) copy-start(f32[8,128,128]{2,1,0:T(8,128)} %param.14) | copy-start | bytes 1572868
  0.6 0.8 copy-start.4
  20.9 17.4 %all-to-all-start.1 = ((f32[4,136,128]{2,1,0:T(8,128)}), f32[4,136,128]{2,1,0:T(8,128)S(1)}, u32[]{:S(2)}, u32[]{:S(2)}) async-start(f32[4,136,128]{2,1,0:T(8,128)} %get-tuple-element.31), calls=%async_computation.1 | async-start | bytes 557056 | tf_op jit(solution)/shard_map/all_to_all | solution.py:344
  39.2 3.5 %copy-start.5 = (f32[256,8]{0,1:T(8,128)S(1)}, f32[256,8]{0,1:T(8,128)}, u32[]{:S(2)}) copy-start(f32[256,8]{0,1:T(8,128)} %param.11) | copy-start | bytes 24580
  39.2 3.5 %copy-start.6 = (f32[1024]{0:T(1024)S(1)}, f32[1024]{0:T(1024)}, u32[]{:S(2)}) copy-start(f32[1024]{0:T(1024)} %param.13) | copy-start | bytes 12292
  39.2 11.7 %all-to-all-start.2 = ((f32[8,128,128]{2,1,0:T(8,128)}), f32[8,128,128]{2,1,0:T(8,128)S(1)}, u32[]{:S(2)}, u32[]{:S(2)}) async-start(f32[8,128,128]{2,1,0:T(8,128)} %get-tuple-element.33), calls=%async_computation.2 | async-start | bytes 1048576 | tf_op jit(solution)/shard_map/all_to_all | solution.py:344
  51.0 2.6 %copy-start.1 = (f32[8,128,128]{2,1,0:T(8,128)}, f32[8,128,128]{2,1,0:T(8,128)S(1)}, u32[]{:S(2)}) copy-start(f32[8,128,128]{2,1,0:T(8,128)S(1)} %all-to-all-done.2.refs_4_.refs_5_) | copy-start | bytes 1572868
  53.6 11.6 %copy-start.2 = (f32[256,1024]{1,0:T(8,128)}, f32[256,1024]{1,0:T(8,128)S(1)}, u32[]{:S(2)}) copy-start(f32[256,1024]{1,0:T(8,128)S(1)} %get-tuple-element.34.refs_3_.refs_2_) | copy-start | bytes 3145732
  65.2 0.8 copy-start.3
  92.2 11.8 %all-to-all-start.6 = ((f32[8,128,128]{2,1,0:T(8,128)}), f32[8,128,128]{2,1,0:T(8,128)S(1)}, u32[]{:S(2)}, u32[]{:S(2)}) async-start(f32[8,128,128]{2,1,0:T(8,128)} %backward_chain_kernel.1), calls=%async_computation.6 | async-start | bytes 1048576 | tf_op jit(solution)/shard_map/all_to_all | solution.py:344

commit v3 on v2

--- a/solution.py
+++ b/solution.py
@@ -39,10 +39,10 @@
     return row, col
 
 
-def state_kernel(io, k_ref, v_ref, decay_ref, out_ref, remain_ref):
-    heads, tokens = decay_ref.shape
+def state_kernel(io, k_ref, v_ref, decay_hbm, out_ref, remain_ref):
+    heads, tokens = decay_hbm.shape
     row, col = square_iota(tokens)
-    decay = decay_ref[...]
+    decay = io.fetch(decay_hbm)[...]
     remain = jnp.exp(token_sums(col > row, decay))
     remain_ref[...] = remain
     closing = jnp.sum(decay, axis=1, keepdims=True)
@@ -54,7 +54,7 @@
         io.send(h)
 
 
-def forward_total_kernel(io, parts_ref, total_ref, factor_ref):
+def forward_total_kernel(io, unread, parts_ref, total_ref, factor_ref):
     members = parts_ref.shape[0]
     carried = parts_ref[0, 0:HD, :]
     length = parts_ref[0, HD : HD + 8, :]
@@ -87,7 +87,7 @@
             carried = factor_ref[m, 0:1, :] * carried + parts_ref[m, 0:HD, :]
 
 
-def backward_total_kernel(io, parts_ref, factor_ref, total_ref):
+def backward_total_kernel(io, unread, also_unread, parts_ref, factor_ref, total_ref):
     members = parts_ref.shape[0]
     returned = parts_ref[members - 1]
     for m in range(members - 2, -1, -1):
@@ -110,35 +110,38 @@
             returned = factor_ref[m, 0:1, :] * returned + parts_ref[m]
 
 
-def running_tables(decay, causal):
-    rows = dot(decay, causal.astype(F32), NT, lax.Precision.HIGHEST)
-    return token_sums(causal, decay), rows
+def running_tables(decay, tokens):
+    row, col = square_iota(tokens)
+    upto = row >= col
+    rows = dot(decay, upto.astype(F32), NT, lax.Precision.HIGHEST)
+    return token_sums(upto, decay), rows, row <= col
 
 
 def head_weights(running, running_rows, h, causal):
-    spread = running[:, h : h + 1] - running_rows[h : h + 1, :]
+    spread = running_rows[h : h + 1, :] - running[:, h : h + 1]
     return jnp.where(causal, jnp.exp(jnp.minimum(spread, 0.0)), 0.0)
 
 
 def within_kernel(
-    io, q_ref, k_ref, v_ref, gate_ref, grad_ref, decay_ref, gain_ref,
-    within_ref, norm_grad_ref, mixing_ref, grown_ref,
+    io, q_ref, k_ref, v_ref, gate_ref, grad_ref, prior_hbm, decay_ref, gain_ref,
+    within_ref, norm_grad_ref, mixing_ref, grown_ref, prior_ref,
 ):
     heads, tokens = decay_ref.shape
-    row, col = square_iota(tokens)
-    causal = row >= col
-    running, running_rows = running_tables(decay_ref[...], causal)
+    place = lax.rem(lax.axis_index("seq"), heads)
+    prior = io.copy(prior_hbm.at[pl.ds(place, 1)], prior_ref)
+    running, running_rows, causal = running_tables(decay_ref[...], tokens)
     grown_ref[...] = jnp.exp(running)
     for h in range(heads):
         io.need(h)
         c = cols(h)
-        scores = dot(q_ref[:, c], k_ref[:, c], NT)
+        scores = dot(k_ref[:, c], q_ref[:, c], NT)
         mixing = (scores * head_weights(running, running_rows, h, causal)).astype(BF16)
         mixing_ref[h] = mixing
-        within_ref[:, c] = dot(mixing, v_ref[:, c], NN)
+        within_ref[:, c] = dot(mixing, v_ref[:, c], TN)
         opened = jax.nn.sigmoid(gate_ref[:, c].astype(F32))
         norm_grad_ref[:, c] = grad_ref[:, c].astype(F32) * gain_ref[:, c] * opened
         io.send(h)
+    prior.wait()
 
 
 def context_kernel(
@@ -166,7 +169,7 @@
 
 
 def gradient_kernel(
-    io, q_ref, norm_grad_ref, sums_ref, context_ref, grown_ref, out_ref, grad_ref, inverse_ref
+    io, q_ref, norm_grad_ref, sums_ref, context_ref, grown_ref, out_ref, grad_ref, inverse_ref,
 ):
     tokens, heads = grown_ref.shape
     total = sums_ref[0]
@@ -209,21 +212,19 @@
     grad_q_ref, grad_k_ref, grad_v_ref,
 ):
     heads, tokens = decay_ref.shape
-    row, col = square_iota(tokens)
-    causal = row >= col
-    running, running_rows = running_tables(decay_ref[...], causal)
+    running, running_rows, causal = running_tables(decay_ref[...], tokens)
     grown = grown_ref[...]
     for h in range(heads):
         io.need(h)
         c = cols(h)
         grad = grad_ref[:, c]
-        scores = dot(grad, v_ref[:, c], NT)
+        scores = dot(v_ref[:, c], grad, NT)
         weights = head_weights(running, running_rows, h, causal)
         grad_mixing = (scores * weights).astype(BF16)
         across = grown[:, h : h + 1] * dot(grad, state_ref[h].astype(BF16), NT)
-        grad_q_ref[:, c] = (dot(grad_mixing, k_ref[:, c], NN) + across).astype(BF16)
-        grad_k_ref[:, c] = dot(grad_mixing, q_ref[:, c], TN)
-        grad_v_ref[:, c] = dot(mixing_ref[h], grad, TN)
+        grad_q_ref[:, c] = (dot(grad_mixing, k_ref[:, c], TN) + across).astype(BF16)
+        grad_k_ref[:, c] = dot(grad_mixing, q_ref[:, c], NN)
+        grad_v_ref[:, c] = dot(mixing_ref[h], grad, NN)
         io.send(h)
 
 
@@ -246,11 +247,23 @@
 
 
 class Stream:
-    def __init__(self, chunks, arrivals, departures):
+    def __init__(self, chunks, arrivals, departures, spare, sem):
         self.chunks, self.arrivals, self.departures = chunks, arrivals, departures
+        self.spare, self.sem = spare, sem
+        if spare is not None:
+            self.early = self.copy(*spare)
         for i in range(chunks):
             for copy in arrivals:
                 copy(i).start()
+
+    def copy(self, source, target):
+        copy = pltpu.make_async_copy(source, target, self.sem)
+        copy.start()
+        return copy
+
+    def fetch(self, source):
+        self.early.wait()
+        return self.spare[1]
 
     def need(self, h):
         if h % PAIR == 0:
@@ -278,7 +291,9 @@
     return lambda i: pltpu.make_async_copy(chunk_of(source, i), chunk_of(target, i), sem.at[n, i])
 
 
-def call(kernel, outs, *args, stream_in=0, stream_out=0, chunks=1, flops=0, limit=16):
+def call(
+    kernel, outs, *args, stream_in=0, raw=0, fetch=False, stream_out=0, chunks=1, flops=0, limit=16
+):
     moved = sum(a.size * a.dtype.itemsize for a in args)
     moved += sum(s.size * s.dtype.itemsize for s in outs)
     inside = pl.BlockSpec(memory_space=pltpu.VMEM)
@@ -295,23 +310,27 @@
             local = scratch[stream_in + j]
             departures.append(copier(local, results[j], scratch[-1], j))
             results[j] = local
-        io = Stream(chunks, arrivals, departures)
+        spare = (ins[stream_in], scratch[stream_in + stream_out]) if fetch else None
+        io = Stream(chunks, arrivals, departures, spare, scratch[-3].at[0])
         kernel(io, *ins, *results)
         io.finish()
 
     streamed = list(args[:stream_in]) + list(outs[:stream_out])
+    if fetch:
+        streamed.append(args[stream_in])
     args = [
-        pltpu.with_memory_space_constraint(a, pltpu.HBM) if j < stream_in else a
+        pltpu.with_memory_space_constraint(a, pltpu.HBM) if j < stream_in + raw else a
         for j, a in enumerate(args)
     ]
     shapes = [pltpu.HBM(s.shape, s.dtype) if j < stream_out else s for j, s in enumerate(outs)]
     return pl.pallas_call(
         body,
         out_shape=tuple(shapes),
-        in_specs=[outside] * stream_in + [inside] * (n - stream_in),
+        in_specs=[outside] * (stream_in + raw) + [inside] * (n - stream_in - raw),
         out_specs=tuple([outside] * stream_out + [inside] * (m - stream_out)),
         scratch_shapes=[pltpu.VMEM(s.shape, s.dtype) for s in streamed]
         + [
+            pltpu.SemaphoreType.DMA((1,)),
             pltpu.SemaphoreType.DMA((max(stream_in, 1), chunks)),
             pltpu.SemaphoreType.DMA((max(stream_out, 1), chunks)),
         ],
@@ -346,21 +365,25 @@
     parts, remain = call(
         state_kernel,
         [shape((heads, HD + 8, HD)), shape((tokens, heads))],
-        key_rows, value_rows, decay, stream_in=2, chunks=chunks, flops=product,
+        key_rows, value_rows, decay,
+        stream_in=2, raw=1, fetch=True, stream_out=1, chunks=chunks, flops=product,
     )
     parts = exchange(parts, "seq", near)
+    within, norm_grad, mixing, grown, prior = call(
+        within_kernel,
+        [
+            shape(wide), shape(wide), shape((heads, tokens, tokens), BF16),
+            shape((tokens, heads)), shape((1, HD, HD)),
+        ],
+        queries, key_rows, value_rows, gate_input, out_grad, prior_state, decay, gain,
+        stream_in=5, raw=1, stream_out=3, chunks=chunks, flops=4 * product, limit=24,
+    )
     total, factor = call(
-        forward_total_kernel, [shape((groups, HD + 8, HD)), shape((heads, 8, HD))], parts
+        forward_total_kernel,
+        [shape((groups, HD + 8, HD)), shape((heads, 8, HD))],
+        within, parts, raw=1,
     )
     total = exchange(total, "seq", far)
-    within, norm_grad, mixing, grown = call(
-        within_kernel,
-        [shape(wide), shape(wide), shape((heads, tokens, tokens), BF16), shape((tokens, heads))],
-        queries, key_rows, value_rows, gate_input, out_grad, decay, gain,
-        stream_in=5, stream_out=3, chunks=chunks, flops=4 * product, limit=24,
-    )
-    place = lax.rem(lax.axis_index("seq"), heads)
-    prior = lax.dynamic_index_in_dim(prior_state, place, 0)
     opening, group_factor = call(
         forward_chain_kernel,
         [shape(states), shape((groups, 8, HD))],
@@ -370,15 +393,14 @@
     context, sums = call(
         context_kernel,
         [shape(wide), shape((peers, 8, tokens))],
-        queries, within, norm_grad, grown, opening,
-        stream_in=3, chunks=chunks, flops=product,
+        queries, within, norm_grad, grown, opening, flops=product,
     )
     sums = exchange(sums, "head")
     parts, grad, inverse = call(
         gradient_kernel,
         [shape(states), shape(wide, BF16), shape((tokens, HD))],
         queries, norm_grad, sums, context, grown,
-        stream_in=2, chunks=chunks, flops=product,
+        stream_out=2, chunks=chunks, flops=product,
     )
     parts = exchange(parts, "seq", near)
     attended, grad_gate = call(
@@ -393,7 +415,11 @@
         queries, key_rows, value_rows, grad, mixing, opening, decay, grown,
         stream_in=6, stream_out=3, chunks=chunks, flops=9 * product, limit=24,
     )
-    (total,) = call(backward_total_kernel, [shape((groups, HD, HD))], parts, factor)
+    (total,) = call(
+        backward_total_kernel,
+        [shape((groups, HD, HD))],
+        attended, part_k, parts, factor, raw=2,
+    )
     total = exchange(total, "seq", far)
     (returned,) = call(
         backward_chain_kernel, [shape(states)], parts, total, factor, group_factor
@@ -403,7 +429,7 @@
         finish_kernel,
         [shape(wide, BF16), shape(wide, BF16)],
         key_rows, value_rows, part_k, part_v, returned, remain,
-        stream_in=4, stream_out=2, chunks=chunks, flops=2 * product,
+        stream_out=2, chunks=chunks, flops=2 * product,
     )
     return attended, grad_query, grad_key, grad_value, grad_gate
 

time: 109 us -> 105 us (0.963)
  blocking collectives: 50.3 us -> 66.6 us
  waiting for transfers between devices: 13.8 us -> 6.64 us
  starting transfers between devices: 14.6 us -> 9.17 us
  Pallas kernels: 26 us -> 20.8 us
  local copies, waits for them, and re-layouts: 1.57 us -> 0.05 us
    all_to_all x4 -> x5, blocking collectives: 50.3 us -> 66.6 us  [exchange(): return lax.all_to_all(value, axis, 0, 0, axis_index_groups=members)]
    all_to_all x3 -> x2, waiting for transfers between devices: 13.8 us -> 6.64 us  [exchange(): return lax.all_to_all(value, axis, 0, 0, axis_index_groups=members)]
    all_to_all x3 -> x2, starting transfers between devices: 14.6 us -> 9.17 us  [exchange(): return lax.all_to_all(value, axis, 0, 0, axis_index_groups=members)]
    pallas_call x11, Pallas kernels: 26 us -> 20.8 us  [call(): pl.pallas_call(body, out_shape=tuple(shapes), in_specs=[outside] * (strea...]
    unnamed x14 -> x22, local copies, waits for them, and re-layouts: 1.57 us -> 0.05 us
  transfers between devices with their start and end apart: 3 -> 2, of which waited for: 2 -> 2; matrix products, arithmetic and copies ran while one was open for 0% -> 0% of each run, Pallas kernels for 12% -> 12%
where the time goes in v3:
time: 105 us; the launch traced here: 104 us
  blocking collectives  66.6 us (63%)
  Pallas kernels  20.8 us (20%)
  starting transfers between devices  9.17 us (9%)
  waiting for transfers between devices  6.64 us (6%)
    all_to_all x5, blocking collectives, exchange(): return lax.all_to_all(value, axis, 0, 0, axis_index_groups=members)  66.6 us
    pallas_call x11, Pallas kernels, call(): pl.pallas_call(body, out_shape=tuple(shapes), in_specs=[outside] * (strea...  20.8 us
    all_to_all x2, starting transfers between devices, exchange(): return lax.all_to_all(value, axis, 0, 0, axis_index_groups=members)  9.17 us
    all_to_all x2, waiting for transfers between devices, exchange(): return lax.all_to_all(value, axis, 0, 0, axis_index_groups=members)  6.64 us
  transfers between devices with their start and end apart: 2, of which 2 were waited for; matrix products, arithmetic and copies ran while one was open for 0% of the time, Pallas kernels for 12%

profile of v3, /device:TPU:8, one launch (start us, length us, event | category | flops | bytes accessed | tf_op | source)
XLA Modules:
  0.0 104.1 jit_solution(7520364033028335608)
XLA Ops:
  0.6 3.6 %state_kernel.1 = (f32[8,136,128]{2,1,0:T(8,128)}, f32[256,8]{1,0:T(8,128)S(1)}) custom-call(bf16[256,1024]{1,0:T(8,128)(2,1)} %refs_0_.13, bf16[256,1024]{1,0:T(8,128)(2,1)} %refs_1_.7, f32[8,256]{1,0:T(8,128)} %bitcast.2), custom_call_target="tpu_custom_call" | custom-call | flops 67108864 | bytes 1622016 | tf_op jit(solution)/shard_map/state_kernel/pallas_call | solution.py:326
  4.2 0.0 copy-start.9
  4.2 5.7 %all-to-all-start = ((f32[8,136,128]{2,1,0:T(8,128)}), f32[8,136,128]{2,1,0:T(8,128)S(1)}, u32[]{:S(2)}, u32[]{:S(2)}) async-start(f32[8,136,128]{2,1,0:T(8,128)} %get-tuple-element.31), calls=%async_computation | async-start | bytes 1114112 | tf_op jit(solution)/shard_map/all_to_all | solution.py:363
  9.9 4.7 %within_kernel.1 = (f32[256,1024]{1,0:T(8,128)}, f32[256,1024]{1,0:T(8,128)}, bf16[8,256,256]{2,1,0:T(8,128)(2,1)}, f32[256,8]{1,0:T(8,128)S(1)}, f32[1,128,128]{2,1,0:T(8,128)S(1)}) custom-call(bf16[256,1024]{1,0:T(8,128)(2,1)} %refs_0_.12, bf16[256,1024]{1,0:T(8,128)(2,1)} %refs_0_.13, bf16[256,1024]{1,0:T(8,128)(2,1)} %refs_1_.7, ...), custom_call_target="tpu_custom_call" | custom-call | flops 268435456 | bytes 6377472 | tf_op jit(solution)/shard_map/within_kernel/pallas_call | solution.py:326
  14.6 5.0 %all-to-all-done.refs_1_.refs_0_ = f32[8,136,128]{2,1,0:T(8,128)S(1)} async-done(((f32[8,136,128]{2,1,0:T(8,128)}), f32[8,136,128]{2,1,0:T(8,128)S(1)}, u32[]{:S(2)}, u32[]{:S(2)}) %all-to-all-start) | async-done | bytes 557088 | tf_op jit(solution)/shard_map/all_to_all | solution.py:363
  19.7 0.1 forward_total_kernel.1
  19.7 18.0 %all_to_all.35.refs_1_ = f32[4,136,128]{2,1,0:T(8,128)S(1)} all-to-all(f32[4,136,128]{2,1,0:T(8,128)S(1)} %get-tuple-element.32), channel_id=1, replica_groups={{0,64,128,192},{8,72,136,200},{16,80,144,208},{24,88,152,216},{32,96,16..., dimensions={0} | all-to-all | bytes 557056 | tf_op jit(solution)/shard_map/all_to_all | solution.py:363
  37.8 0.1 forward_chain_kernel.1
  37.9 0.0 copy-start.1
  37.9 12.9 %all_to_all.36.refs_4_.refs_5_ = f32[8,128,128]{2,1,0:T(8,128)S(1)} all-to-all(f32[8,128,128]{2,1,0:T(8,128)S(1)} %get-tuple-element.35), channel_id=1, replica_groups={{0,8,16,24,32,40,48,56},{64,72,80,88,96,104,112,120},{128,136,144,152,1..., dimensions={0} | all-to-all | bytes 1048576 | tf_op jit(solution)/shard_map/all_to_all | solution.py:363
  50.8 0.8 context_kernel.1
  51.7 8.9 %all_to_all.37.refs_2_ = f32[8,8,256]{2,1,0:T(8,128)S(1)} all-to-all(f32[8,8,256]{2,1,0:T(8,128)S(1)} %get-tuple-element.37), channel_id=1, replica_groups=mesh['seq'=32,'head'=8] {'head'}, dimensions={0} | all-to-all | bytes 131072 | tf_op jit(solution)/shard_map/all_to_all | solution.py:363
  60.6 2.1 %gradient_kernel.1 = (f32[8,128,128]{2,1,0:T(8,128)}, bf16[256,1024]{1,0:T(8,128)(2,1)}, f32[256,128]{1,0:T(8,128)S(1)}) custom-call(bf16[256,1024]{1,0:T(8,128)(2,1)S(1)} %copy-done.1, f32[256,1024]{1,0:T(8,128)S(1)} %copy-done, f32[8,8,256]{2,1,0:T(8,128)S(1)} %all_to_all.37.refs_2_, f32[256,1024]{1,0:T(8,128)S(1)} %get-tuple-element.36.refs_3_.refs_2_, ...), custom_call_target="tpu_custom_call" | custom-call | flops 67108864 | bytes 3874816 | tf_op jit(solution)/shard_map/gradient_kernel/pallas_call | solution.py:326
  62.7 3.5 %all-to-all-start.4 = ((f32[8,128,128]{2,1,0:T(8,128)}), f32[8,128,128]{2,1,0:T(8,128)S(1)}, u32[]{:S(2)}, u32[]{:S(2)}) async-start(f32[8,128,128]{2,1,0:T(8,128)} %get-tuple-element.45), calls=%async_computation.4 | async-start | bytes 1048576 | tf_op jit(solution)/shard_map/all_to_all | solution.py:363
  66.2 2.7 %gate_kernel.1 = (bf16[256,1024]{1,0:T(8,128)(2,1)}, bf16[256,1024]{1,0:T(8,128)(2,1)}) custom-call(bf16[256,1024]{1,0:T(8,128)(2,1)} %refs_0_.11, f32[256,1024]{1,0:T(8,128)} %get-tuple-element.28.refs_2_.refs_1_, f32[256,1024]{1,0:T(8,128)} %copy-done.7, f32[1,1024]{1,0:T(1,128)S(1)} %bitcast.6, f32[256,128]{1,0:T(8,128)S(1)} %get-tuple-element.38.refs_4_), custom_call_target="tpu_custom_call" | custom-call | flops 67108864 | bytes 3805184 | tf_op jit(solution)/shard_map/gate_kernel/pallas_call | solution.py:326
  68.9 5.2 %local_backward_kernel.1 = (bf16[256,1024]{1,0:T(8,128)(2,1)}, f32[256,1024]{1,0:T(8,128)}, f32[256,1024]{1,0:T(8,128)}) custom-call(bf16[256,1024]{1,0:T(8,128)(2,1)} %refs_0_.12, bf16[256,1024]{1,0:T(8,128)(2,1)} %refs_0_.13, bf16[256,1024]{1,0:T(8,128)(2,1)} %refs_1_.7, bf16[256,1024]{1,0:T(8,128)(2,1)} %get-tuple-element.40.refs_3_, ...), custom_call_target="tpu_custom_call" | custom-call | flops 603979776 | bytes 6307840 | tf_op jit(solution)/shard_map/local_backward_kernel/pallas_call | solution.py:326
  74.1 1.6 %all-to-all-done.4.refs_2_.refs_0_ = f32[8,128,128]{2,1,0:T(8,128)S(1)} async-done(((f32[8,128,128]{2,1,0:T(8,128)}), f32[8,128,128]{2,1,0:T(8,128)S(1)}, u32[]{:S(2)}, u32[]{:S(2)}) %all-to-all-start.4) | async-done | bytes 524320 | tf_op jit(solution)/shard_map/all_to_all | solution.py:363
  75.7 0.1 backward_total_kernel.1
  75.8 14.2 %all_to_all.38.refs_1_ = f32[4,128,128]{2,1,0:T(8,128)S(1)} all-to-all(f32[4,128,128]{2,1,0:T(8,128)S(1)} %backward_total_kernel.1), channel_id=1, replica_groups={{0,64,128,192},{8,72,136,200},{16,80,144,208},{24,88,152,216},{32,96,16..., dimensions={0} | all-to-all | bytes 524288 | tf_op jit(solution)/shard_map/all_to_all | solution.py:363
  90.0 0.1 backward_chain_kernel.1
  90.1 0.0 copy-start.2
  90.1 0.0 copy-start.3
  90.1 12.6 %all_to_all.39.refs_4_ = f32[8,128,128]{2,1,0:T(8,128)S(1)} all-to-all(f32[8,128,128]{2,1,0:T(8,128)S(1)} %backward_chain_kernel.1), channel_id=1, replica_groups={{0,8,16,24,32,40,48,56},{64,72,80,88,96,104,112,120},{128,136,144,152,1..., dimensions={0} | all-to-all | bytes 1048576 | tf_op jit(solution)/shard_map/all_to_all | solution.py:363
  102.7 1.4 %finish_kernel.1 = (bf16[256,1024]{1,0:T(8,128)(2,1)}, bf16[256,1024]{1,0:T(8,128)(2,1)}) custom-call(bf16[256,1024]{1,0:T(8,128)(2,1)S(1)} %copy-done.2, bf16[256,1024]{1,0:T(8,128)(2,1)S(1)} %copy-done.3, f32[256,1024]{1,0:T(8,128)S(1)} %copy-done.6, f32[256,1024]{1,0:T(8,128)S(1)} %copy-done.8, f32[8,128,128]{2,1,0:T(8,128)S(1)} %all_to_all.39.refs_4_, ...), custom_call_target="tpu_custom_call" | custom-call | flops 134217728 | bytes 4726784 | tf_op jit(solution)/shard_map/finish_kernel/pallas_call | solution.py:326
  (18 shorter events, 0.0 us)
Async XLA Ops:
  4.2 5.7 %copy-start.9 = (f32[256,8]{0,1:T(8,128)S(1)}, f32[256,8]{0,1:T(8,128)}, u32[]{:S(2)}) copy-start(f32[256,8]{0,1:T(8,128)} %param.11) | copy-start | bytes 24580
  4.2 5.7 %copy-start.10 = (f32[1024]{0:T(1024)S(1)}, f32[1024]{0:T(1024)}, u32[]{:S(2)}) copy-start(f32[1024]{0:T(1024)} %param.13) | copy-start | bytes 12292
  4.2 15.4 %all-to-all-start = ((f32[8,136,128]{2,1,0:T(8,128)}), f32[8,136,128]{2,1,0:T(8,128)S(1)}, u32[]{:S(2)}, u32[]{:S(2)}) async-start(f32[8,136,128]{2,1,0:T(8,128)} %get-tuple-element.31), calls=%async_computation | async-start | bytes 1114112 | tf_op jit(solution)/shard_map/all_to_all | solution.py:363
  19.6 31.2 %copy-start.5 = (f32[256,1024]{1,0:T(8,128)S(1)}, f32[256,1024]{1,0:T(8,128)}, u32[]{:S(2)}) copy-start(f32[256,1024]{1,0:T(8,128)} %get-tuple-element.29.refs_0_.refs_1_) | copy-start | bytes 3145732
  37.8 13.0 %copy-start = (f32[256,1024]{1,0:T(8,128)S(1)}, f32[256,1024]{1,0:T(8,128)}, u32[]{:S(2)}) copy-start(f32[256,1024]{1,0:T(8,128)} %get-tuple-element.28.refs_2_.refs_1_) | copy-start | bytes 3145732
  37.9 12.9 %copy-start.1 = (bf16[256,1024]{1,0:T(8,128)(2,1)S(1)}, bf16[256,1024]{1,0:T(8,128)(2,1)}, u32[]{:S(2)}) copy-start(bf16[256,1024]{1,0:T(8,128)(2,1)} %refs_0_.12) | copy-start | bytes 1572868
  50.8 0.9 copy-start.4
  51.7 11.0 %copy-start.7 = (f32[256,1024]{1,0:T(8,128)}, f32[256,1024]{1,0:T(8,128)S(1)}, u32[]{:S(2)}) copy-start(f32[256,1024]{1,0:T(8,128)S(1)} %get-tuple-element.36.refs_3_.refs_2_) | copy-start | bytes 3145732
  62.7 13.0 %all-to-all-start.4 = ((f32[8,128,128]{2,1,0:T(8,128)}), f32[8,128,128]{2,1,0:T(8,128)S(1)}, u32[]{:S(2)}, u32[]{:S(2)}) async-start(f32[8,128,128]{2,1,0:T(8,128)} %get-tuple-element.45), calls=%async_computation.4 | async-start | bytes 1048576 | tf_op jit(solution)/shard_map/all_to_all | solution.py:363
  75.7 27.0 %copy-start.8 = (f32[256,1024]{1,0:T(8,128)S(1)}, f32[256,1024]{1,0:T(8,128)}, u32[]{:S(2)}) copy-start(f32[256,1024]{1,0:T(8,128)} %get-tuple-element.44.refs_3_) | copy-start | bytes 3145732
  90.0 12.7 %copy-start.6 = (f32[256,1024]{1,0:T(8,128)S(1)}, f32[256,1024]{1,0:T(8,128)}, u32[]{:S(2)}) copy-start(f32[256,1024]{1,0:T(8,128)} %get-tuple-element.43.refs_1_.refs_2_) | copy-start | bytes 3145732
  90.1 12.6 %copy-start.2 = (bf16[256,1024]{1,0:T(8,128)(2,1)S(1)}, bf16[256,1024]{1,0:T(8,128)(2,1)}, u32[]{:S(2)}) copy-start(bf16[256,1024]{1,0:T(8,128)(2,1)} %refs_0_.13) | copy-start | bytes 1572868
  90.1 12.6 %copy-start.3 = (bf16[256,1024]{1,0:T(8,128)(2,1)S(1)}, bf16[256,1024]{1,0:T(8,128)(2,1)}, u32[]{:S(2)}) copy-start(bf16[256,1024]{1,0:T(8,128)(2,1)} %refs_1_.7) | copy-start | bytes 1572868

commit v4 on v3

--- a/solution.py
+++ b/solution.py
@@ -30,7 +30,17 @@
 
 
 def token_sums(table, decay):
-    return dot(table.astype(F32), decay, NT, lax.Precision.HIGHEST)
+    heads = decay.shape[0]
+    sums = dot(table.astype(F32).astype(BF16), thirds(decay), NT)
+    return sums[:, 0:heads] + sums[:, heads : 2 * heads] + sums[:, 2 * heads : 3 * heads]
+
+
+def thirds(decay):
+    upper = decay.astype(BF16).astype(F32)
+    rest = decay - upper
+    middle = rest.astype(BF16).astype(F32)
+    lower = rest - middle
+    return jnp.concatenate([upper, middle, lower], axis=0).astype(BF16)
 
 
 def square_iota(n):
@@ -87,7 +97,7 @@
             carried = factor_ref[m, 0:1, :] * carried + parts_ref[m, 0:HD, :]
 
 
-def backward_total_kernel(io, unread, also_unread, parts_ref, factor_ref, total_ref):
+def backward_total_kernel(io, unread, parts_ref, factor_ref, total_ref):
     members = parts_ref.shape[0]
     returned = parts_ref[members - 1]
     for m in range(members - 2, -1, -1):
@@ -113,7 +123,9 @@
 def running_tables(decay, tokens):
     row, col = square_iota(tokens)
     upto = row >= col
-    rows = dot(decay, upto.astype(F32), NT, lax.Precision.HIGHEST)
+    heads = decay.shape[0]
+    sums = dot(thirds(decay), upto.astype(F32).astype(BF16), NT)
+    rows = sums[0:heads] + sums[heads : 2 * heads] + sums[2 * heads : 3 * heads]
     return token_sums(upto, decay), rows, row <= col
 
 
@@ -124,13 +136,14 @@
 
 def within_kernel(
     io, q_ref, k_ref, v_ref, gate_ref, grad_ref, prior_hbm, decay_ref, gain_ref,
-    within_ref, norm_grad_ref, mixing_ref, grown_ref, prior_ref,
+    within_ref, norm_grad_ref, mixing_ref, query_ref, grown_ref, prior_ref,
 ):
     heads, tokens = decay_ref.shape
     place = lax.rem(lax.axis_index("seq"), heads)
     prior = io.copy(prior_hbm.at[pl.ds(place, 1)], prior_ref)
     running, running_rows, causal = running_tables(decay_ref[...], tokens)
-    grown_ref[...] = jnp.exp(running)
+    grown = jnp.exp(running)
+    grown_ref[...] = grown
     for h in range(heads):
         io.need(h)
         c = cols(h)
@@ -138,6 +151,8 @@
         mixing = (scores * head_weights(running, running_rows, h, causal)).astype(BF16)
         mixing_ref[h] = mixing
         within_ref[:, c] = dot(mixing, v_ref[:, c], TN)
+        scaled = (q_ref[:, c].astype(F32) * grown[:, h : h + 1]).astype(BF16)
+        query_ref[h] = scaled.T
         opened = jax.nn.sigmoid(gate_ref[:, c].astype(F32))
         norm_grad_ref[:, c] = grad_ref[:, c].astype(F32) * gain_ref[:, c] * opened
         io.send(h)
@@ -160,8 +175,8 @@
         squares += context * context
         products += context * norm_grad_ref[:, c]
     ones = jnp.ones((8, HD), F32)
-    square_rows = dot(ones, squares, NT, lax.Precision.HIGHEST)
-    product_rows = dot(ones, products, NT, lax.Precision.HIGHEST)
+    square_rows = dot(ones, squares, NT, lax.Precision.HIGHEST)[0:2]
+    product_rows = dot(ones, products, NT, lax.Precision.HIGHEST)[0:2]
     first = lax.broadcasted_iota(jnp.int32, square_rows.shape, 0) == 0
     both = jnp.where(first, square_rows, product_rows)
     for p in range(sums_ref.shape[0]):
@@ -169,55 +184,46 @@
 
 
 def gradient_kernel(
-    io, q_ref, norm_grad_ref, sums_ref, context_ref, grown_ref, out_ref, grad_ref, inverse_ref,
-):
-    tokens, heads = grown_ref.shape
+    io, query_ref, norm_grad_ref, sums_ref, context_ref, out_ref, inverse_ref, slope_ref
+):
+    heads = query_ref.shape[0]
     total = sums_ref[0]
     for p in range(1, sums_ref.shape[0]):
         total = total + sums_ref[p]
-    pick = lax.broadcasted_iota(jnp.int32, (8, HD), 0)
+    pick = lax.broadcasted_iota(jnp.int32, (2, HD), 0)
     square = dot(total, (pick == 0).astype(F32), TN, lax.Precision.HIGHEST)
     product = dot(total, (pick == 1).astype(F32), TN, lax.Precision.HIGHEST)
     inverse = lax.rsqrt(square / D + epsilon)
+    slope = inverse * inverse * inverse * product / D
     inverse_ref[...] = inverse
-    slope = inverse * inverse * inverse * product / D
-    grown = grown_ref[...]
-    for h in range(heads):
-        io.need(h)
+    slope_ref[...] = slope
+    for h in range(heads):
         c = cols(h)
         grad = (inverse * norm_grad_ref[:, c] - context_ref[:, c] * slope).astype(BF16)
-        grad_ref[:, c] = grad
-        scaled = (q_ref[:, c].astype(F32) * grown[:, h : h + 1]).astype(BF16)
-        out_ref[h] = dot(scaled, grad, TN)
+        out_ref[h] = dot(query_ref[h], grad, NN)
         io.send(h)
 
 
-def gate_kernel(
-    io, gate_ref, norm_grad_ref, context_ref, gain_ref, inverse_ref, attended_ref, grad_gate_ref
-):
-    heads = context_ref.shape[1] // HD
-    inverse = inverse_ref[...]
-    for h in range(heads):
-        io.need(h)
-        c = cols(h)
-        opened = jax.nn.sigmoid(gate_ref[:, c].astype(F32))
-        normed = context_ref[:, c] * inverse
-        attended_ref[:, c] = (normed * gain_ref[:, c] * opened).astype(BF16)
-        grad_gate_ref[:, c] = (norm_grad_ref[:, c] * normed * (1.0 - opened)).astype(BF16)
-        io.send(h)
-
-
 def local_backward_kernel(
-    io, q_ref, k_ref, v_ref, grad_ref, mixing_ref, state_ref, decay_ref, grown_ref,
-    grad_q_ref, grad_k_ref, grad_v_ref,
+    io, q_ref, k_ref, v_ref, gate_ref, norm_grad_ref, context_ref, mixing_ref, state_ref,
+    decay_ref, grown_ref, gain_ref, inverse_ref, slope_ref,
+    attended_ref, grad_gate_ref, grad_q_ref, grad_k_ref, grad_v_ref,
 ):
     heads, tokens = decay_ref.shape
     running, running_rows, causal = running_tables(decay_ref[...], tokens)
     grown = grown_ref[...]
+    inverse = inverse_ref[...]
+    slope = slope_ref[...]
     for h in range(heads):
         io.need(h)
         c = cols(h)
-        grad = grad_ref[:, c]
+        context = context_ref[:, c]
+        norm_grad = norm_grad_ref[:, c]
+        opened = jax.nn.sigmoid(gate_ref[:, c].astype(F32))
+        normed = context * inverse
+        attended_ref[:, c] = (normed * gain_ref[:, c] * opened).astype(BF16)
+        grad_gate_ref[:, c] = (norm_grad * normed * (1.0 - opened)).astype(BF16)
+        grad = (inverse * norm_grad - context * slope).astype(BF16)
         scores = dot(v_ref[:, c], grad, NT)
         weights = head_weights(running, running_rows, h, causal)
         grad_mixing = (scores * weights).astype(BF16)
@@ -369,14 +375,14 @@
         stream_in=2, raw=1, fetch=True, stream_out=1, chunks=chunks, flops=product,
     )
     parts = exchange(parts, "seq", near)
-    within, norm_grad, mixing, grown, prior = call(
+    within, norm_grad, mixing, scaled, grown, prior = call(
         within_kernel,
         [
             shape(wide), shape(wide), shape((heads, tokens, tokens), BF16),
-            shape((tokens, heads)), shape((1, HD, HD)),
+            shape((heads, HD, tokens), BF16), shape((tokens, heads)), shape((1, HD, HD)),
         ],
         queries, key_rows, value_rows, gate_input, out_grad, prior_state, decay, gain,
-        stream_in=5, raw=1, stream_out=3, chunks=chunks, flops=4 * product, limit=24,
+        stream_in=5, raw=1, stream_out=4, chunks=chunks, flops=4 * product, limit=24,
     )
     total, factor = call(
         forward_total_kernel,
@@ -392,33 +398,28 @@
     opening = exchange(opening, "seq", near)
     context, sums = call(
         context_kernel,
-        [shape(wide), shape((peers, 8, tokens))],
+        [shape(wide), shape((peers, 2, tokens))],
         queries, within, norm_grad, grown, opening, flops=product,
     )
     sums = exchange(sums, "head")
-    parts, grad, inverse = call(
+    parts, inverse, slope = call(
         gradient_kernel,
-        [shape(states), shape(wide, BF16), shape((tokens, HD))],
-        queries, norm_grad, sums, context, grown,
-        stream_out=2, chunks=chunks, flops=product,
+        [shape(states), shape((tokens, HD)), shape((tokens, HD))],
+        scaled, norm_grad, sums, context,
+        stream_out=1, chunks=chunks, flops=product,
     )
     parts = exchange(parts, "seq", near)
-    attended, grad_gate = call(
-        gate_kernel,
-        [shape(wide, BF16), shape(wide, BF16)],
-        gate_input, norm_grad, context, gain, inverse,
-        stream_in=3, stream_out=2, chunks=chunks, flops=product,
-    )
-    grad_query, part_k, part_v = call(
+    attended, grad_gate, grad_query, part_k, part_v = call(
         local_backward_kernel,
-        [shape(wide, BF16), shape(wide), shape(wide)],
-        queries, key_rows, value_rows, grad, mixing, opening, decay, grown,
-        stream_in=6, stream_out=3, chunks=chunks, flops=9 * product, limit=24,
+        [shape(wide, BF16), shape(wide, BF16), shape(wide, BF16), shape(wide), shape(wide)],
+        queries, key_rows, value_rows, gate_input, norm_grad, context, mixing, opening,
+        decay, grown, gain, inverse, slope,
+        stream_in=8, stream_out=5, chunks=chunks, flops=9 * product, limit=32,
     )
     (total,) = call(
         backward_total_kernel,
         [shape((groups, HD, HD))],
-        attended, part_k, parts, factor, raw=2,
+        part_k, parts, factor, raw=1,
     )
     total = exchange(total, "seq", far)
     (returned,) = call(

time: 105 us -> 104 us (level)
  Pallas kernels: 20.8 us -> 18.4 us
  waiting for transfers between devices: 6.64 us -> 8.53 us
    pallas_call x11 -> x10, Pallas kernels: 20.8 us -> 18.4 us  [call(): pl.pallas_call(body, out_shape=tuple(shapes), in_specs=[outside] * (strea...]
    all_to_all x2, waiting for transfers between devices: 6.64 us -> 8.53 us  [exchange(): return lax.all_to_all(value, axis, 0, 0, axis_index_groups=members)]
  transfers between devices with their start and end apart: 2 -> 2, of which waited for: 2 -> 2; matrix products, arithmetic and copies ran while one was open for 0% -> 0% of each run, Pallas kernels for 12% -> 10%
where the time goes in v4:
time: 104 us; the launch traced here: 103 us
  blocking collectives  66.4 us (64%)
  Pallas kernels  18.4 us (18%)
  starting transfers between devices  9.17 us (9%)
  waiting for transfers between devices  8.53 us (8%)
    all_to_all x5, blocking collectives, exchange(): return lax.all_to_all(value, axis, 0, 0, axis_index_groups=members)  66.4 us
    pallas_call x10, Pallas kernels, call(): pl.pallas_call(body, out_shape=tuple(shapes), in_specs=[outside] * (strea...  18.4 us
    all_to_all x2, starting transfers between devices, exchange(): return lax.all_to_all(value, axis, 0, 0, axis_index_groups=members)  9.17 us
    all_to_all x2, waiting for transfers between devices, exchange(): return lax.all_to_all(value, axis, 0, 0, axis_index_groups=members)  8.53 us
  transfers between devices with their start and end apart: 2, of which 2 were waited for; matrix products, arithmetic and copies ran while one was open for 0% of the time, Pallas kernels for 10%

profile of v4, /device:TPU:8, one launch (start us, length us, event | category | flops | bytes accessed | tf_op | source)
XLA Modules:
  0.0 103.4 jit_solution(10655511949124274793)
XLA Ops:
  0.6 3.5 %state_kernel.1 = (f32[8,136,128]{2,1,0:T(8,128)}, f32[256,8]{1,0:T(8,128)S(1)}) custom-call(bf16[256,1024]{1,0:T(8,128)(2,1)} %refs_0_.9, bf16[256,1024]{1,0:T(8,128)(2,1)} %refs_1_.7, f32[8,256]{1,0:T(8,128)} %bitcast.2), custom_call_target="tpu_custom_call" | custom-call | flops 67108864 | bytes 1622016 | tf_op jit(solution)/shard_map/state_kernel/pallas_call | solution.py:332
  4.1 0.0 copy-start.10
  4.1 0.0 copy-start.11
  4.1 5.7 %all-to-all-start = ((f32[8,136,128]{2,1,0:T(8,128)}), f32[8,136,128]{2,1,0:T(8,128)S(1)}, u32[]{:S(2)}, u32[]{:S(2)}) async-start(f32[8,136,128]{2,1,0:T(8,128)} %get-tuple-element.32), calls=%async_computation | async-start | bytes 1114112 | tf_op jit(solution)/shard_map/all_to_all | solution.py:369
  9.8 5.1 %within_kernel.1 = (f32[256,1024]{1,0:T(8,128)}, f32[256,1024]{1,0:T(8,128)}, bf16[8,256,256]{2,1,0:T(8,128)(2,1)}, bf16[8,128,256]{2,1,0:T(8,128)(2,1)}, f32[25...) custom-call(bf16[256,1024]{1,0:T(8,128)(2,1)} %refs_0_.8, bf16[256,1024]{1,0:T(8,128)(2,1)} %refs_0_.9, ...), custom_call_target="tpu_custom_call" | custom-call | flops 268435456 | bytes 6901760 | tf_op jit(solution)/shard_map/within_kernel/pallas_call | solution.py:332
  14.9 4.6 %all-to-all-done.refs_1_.refs_0_ = f32[8,136,128]{2,1,0:T(8,128)S(1)} async-done(((f32[8,136,128]{2,1,0:T(8,128)}), f32[8,136,128]{2,1,0:T(8,128)S(1)}, u32[]{:S(2)}, u32[]{:S(2)}) %all-to-all-start) | async-done | bytes 557088 | tf_op jit(solution)/shard_map/all_to_all | solution.py:369
  19.5 0.1 forward_total_kernel.1
  19.6 18.0 %all_to_all.35.refs_1_ = f32[4,136,128]{2,1,0:T(8,128)S(1)} all-to-all(f32[4,136,128]{2,1,0:T(8,128)S(1)} %get-tuple-element.33), channel_id=1, replica_groups={{0,64,128,192},{8,72,136,200},{16,80,144,208},{24,88,152,216},{32,96,16..., dimensions={0} | all-to-all | bytes 557056 | tf_op jit(solution)/shard_map/all_to_all | solution.py:369
  37.7 0.1 forward_chain_kernel.1
  37.8 0.0 copy-start.4
  37.8 12.9 %all_to_all.36.refs_4_.refs_7_ = f32[8,128,128]{2,1,0:T(8,128)S(1)} all-to-all(f32[8,128,128]{2,1,0:T(8,128)S(1)} %get-tuple-element.36), channel_id=1, replica_groups={{0,8,16,24,32,40,48,56},{64,72,80,88,96,104,112,120},{128,136,144,152,1..., dimensions={0} | all-to-all | bytes 1048576 | tf_op jit(solution)/shard_map/all_to_all | solution.py:369
  50.7 0.0 copy-start.9
  50.7 0.9 context_kernel.1
  51.6 8.6 %all_to_all.37.refs_2_ = f32[8,2,256]{2,1,0:T(2,128)S(1)} all-to-all(f32[8,2,256]{2,1,0:T(2,128)S(1)} %get-tuple-element.40), channel_id=1, replica_groups=mesh['seq'=32,'head'=8] {'head'}, dimensions={0} | all-to-all | bytes 32768 | tf_op jit(solution)/shard_map/all_to_all | solution.py:369
  60.2 1.6 %gradient_kernel.1 = (f32[8,128,128]{2,1,0:T(8,128)}, f32[256,128]{1,0:T(8,128)S(1)}, f32[256,128]{1,0:T(8,128)S(1)}) custom-call(bf16[8,128,256]{2,1,0:T(8,128)(2,1)S(1)} %copy-done.9, f32[256,1024]{1,0:T(8,128)S(1)} %copy-done, f32[8,2,256]{2,1,0:T(2,128)S(1)} %all_to_all.37.refs_2_, f32[256,1024]{1,0:T(8,128)S(1)} %get-tuple-element.37.refs_3_.refs_5_), custom_call_target="tpu_custom_call" | custom-call | flops 67108864 | bytes 3424256 | tf_op jit(solution)/shard_map/gradient_kernel/pallas_call | solution.py:332
  61.8 3.5 %all-to-all-start.4 = ((f32[8,128,128]{2,1,0:T(8,128)}), f32[8,128,128]{2,1,0:T(8,128)S(1)}, u32[]{:S(2)}, u32[]{:S(2)}) async-start(f32[8,128,128]{2,1,0:T(8,128)} %get-tuple-element.47), calls=%async_computation.4 | async-start | bytes 1048576 | tf_op jit(solution)/shard_map/all_to_all | solution.py:369
  65.3 5.7 %local_backward_kernel.1 = (bf16[256,1024]{1,0:T(8,128)(2,1)}, bf16[256,1024]{1,0:T(8,128)(2,1)}, bf16[256,1024]{1,0:T(8,128)(2,1)}, f32[256,1024]{1,0:T(8,128)}, f32[256,1024]{1,0:T(8,128)}) custom-call(bf16[256,1024]{1,0:T(8,128)(2,1)} %refs_0_.8, bf16[256,1024]{1,0:T(8,128)(2,1)} %refs_0_.9, bf16[256,1024]{1,0:T(8,128)(2,1)} %refs_1_.7, ...), custom_call_target="tpu_custom_call" | custom-call | flops 603979776 | bytes 9719808 | tf_op jit(solution)/shard_map/local_backward_kernel/pallas_call | solution.py:332
  71.0 3.9 %all-to-all-done.4.refs_1_.refs_0_ = f32[8,128,128]{2,1,0:T(8,128)S(1)} async-done(((f32[8,128,128]{2,1,0:T(8,128)}), f32[8,128,128]{2,1,0:T(8,128)S(1)}, u32[]{:S(2)}, u32[]{:S(2)}) %all-to-all-start.4) | async-done | bytes 524320 | tf_op jit(solution)/shard_map/all_to_all | solution.py:369
  74.9 0.1 backward_total_kernel.1
  75.0 14.2 %all_to_all.38.refs_1_ = f32[4,128,128]{2,1,0:T(8,128)S(1)} all-to-all(f32[4,128,128]{2,1,0:T(8,128)S(1)} %backward_total_kernel.1), channel_id=1, replica_groups={{0,64,128,192},{8,72,136,200},{16,80,144,208},{24,88,152,216},{32,96,16..., dimensions={0} | all-to-all | bytes 524288 | tf_op jit(solution)/shard_map/all_to_all | solution.py:369
  89.2 0.1 backward_chain_kernel.1
  89.3 0.0 copy-start.1
  89.4 12.6 %all_to_all.39.refs_4_ = f32[8,128,128]{2,1,0:T(8,128)S(1)} all-to-all(f32[8,128,128]{2,1,0:T(8,128)S(1)} %backward_chain_kernel.1), channel_id=1, replica_groups={{0,8,16,24,32,40,48,56},{64,72,80,88,96,104,112,120},{128,136,144,152,1..., dimensions={0} | all-to-all | bytes 1048576 | tf_op jit(solution)/shard_map/all_to_all | solution.py:369
  102.0 1.4 %finish_kernel.1 = (bf16[256,1024]{1,0:T(8,128)(2,1)}, bf16[256,1024]{1,0:T(8,128)(2,1)}) custom-call(bf16[256,1024]{1,0:T(8,128)(2,1)S(1)} %copy-done.1, bf16[256,1024]{1,0:T(8,128)(2,1)S(1)} %copy-done.2, f32[256,1024]{1,0:T(8,128)S(1)} %copy-done.6, f32[256,1024]{1,0:T(8,128)S(1)} %copy-done.8, f32[8,128,128]{2,1,0:T(8,128)S(1)} %all_to_all.39.refs_4_, ...), custom_call_target="tpu_custom_call" | custom-call | flops 134217728 | bytes 4726784 | tf_op jit(solution)/shard_map/finish_kernel/pallas_call | solution.py:332
  (19 shorter events, 0.0 us)
Async XLA Ops:
  4.1 5.7 %copy-start.10 = (f32[256,8]{0,1:T(8,128)S(1)}, f32[256,8]{0,1:T(8,128)}, u32[]{:S(2)}) copy-start(f32[256,8]{0,1:T(8,128)} %param.11) | copy-start | bytes 24580
  4.1 5.7 %copy-start.11 = (f32[1024]{0:T(1024)S(1)}, f32[1024]{0:T(1024)}, u32[]{:S(2)}) copy-start(f32[1024]{0:T(1024)} %param.13) | copy-start | bytes 12292
  4.1 15.4 %all-to-all-start = ((f32[8,136,128]{2,1,0:T(8,128)}), f32[8,136,128]{2,1,0:T(8,128)S(1)}, u32[]{:S(2)}, u32[]{:S(2)}) async-start(f32[8,136,128]{2,1,0:T(8,128)} %get-tuple-element.32), calls=%async_computation | async-start | bytes 1114112 | tf_op jit(solution)/shard_map/all_to_all | solution.py:369
  19.5 31.2 %copy-start.5 = (f32[256,1024]{1,0:T(8,128)S(1)}, f32[256,1024]{1,0:T(8,128)}, u32[]{:S(2)}) copy-start(f32[256,1024]{1,0:T(8,128)} %get-tuple-element.30.refs_0_.refs_1_) | copy-start | bytes 3145732
  37.7 13.0 %copy-start = (f32[256,1024]{1,0:T(8,128)S(1)}, f32[256,1024]{1,0:T(8,128)}, u32[]{:S(2)}) copy-start(f32[256,1024]{1,0:T(8,128)} %get-tuple-element.29.refs_2_.refs_1_.refs_4_) | copy-start | bytes 3145732
  37.8 12.9 %copy-start.4 = (bf16[256,1024]{1,0:T(8,128)(2,1)S(1)}, bf16[256,1024]{1,0:T(8,128)(2,1)}, u32[]{:S(2)}) copy-start(bf16[256,1024]{1,0:T(8,128)(2,1)} %refs_0_.8) | copy-start | bytes 1572868
  50.7 0.9 copy-start.3
  50.7 9.5 %copy-start.9 = (bf16[8,128,256]{2,1,0:T(8,128)(2,1)S(1)}, bf16[8,128,256]{2,1,0:T(8,128)(2,1)}, u32[]{:S(2)}) copy-start(bf16[8,128,256]{2,1,0:T(8,128)(2,1)} %get-tuple-element.39.refs_0_) | copy-start | bytes 1572868
  51.6 10.2 %copy-start.7 = (f32[256,1024]{1,0:T(8,128)}, f32[256,1024]{1,0:T(8,128)S(1)}, u32[]{:S(2)}) copy-start(f32[256,1024]{1,0:T(8,128)S(1)} %get-tuple-element.37.refs_3_.refs_5_) | copy-start | bytes 3145732
  61.8 13.1 %all-to-all-start.4 = ((f32[8,128,128]{2,1,0:T(8,128)}), f32[8,128,128]{2,1,0:T(8,128)S(1)}, u32[]{:S(2)}, u32[]{:S(2)}) async-start(f32[8,128,128]{2,1,0:T(8,128)} %get-tuple-element.47), calls=%async_computation.4 | async-start | bytes 1048576 | tf_op jit(solution)/shard_map/all_to_all | solution.py:369
  74.9 27.0 %copy-start.8 = (f32[256,1024]{1,0:T(8,128)S(1)}, f32[256,1024]{1,0:T(8,128)}, u32[]{:S(2)}) copy-start(f32[256,1024]{1,0:T(8,128)} %get-tuple-element.46.refs_3_) | copy-start | bytes 3145732
  89.2 12.7 %copy-start.6 = (f32[256,1024]{1,0:T(8,128)S(1)}, f32[256,1024]{1,0:T(8,128)}, u32[]{:S(2)}) copy-start(f32[256,1024]{1,0:T(8,128)} %get-tuple-element.45.refs_0_.refs_2_) | copy-start | bytes 3145732
  89.3 12.6 %copy-start.1 = (bf16[256,1024]{1,0:T(8,128)(2,1)S(1)}, bf16[256,1024]{1,0:T(8,128)(2,1)}, u32[]{:S(2)}) copy-start(bf16[256,1024]{1,0:T(8,128)(2,1)} %refs_0_.9) | copy-start | bytes 1572868
  89.4 12.6 %copy-start.2 = (bf16[256,1024]{1,0:T(8,128)(2,1)S(1)}, bf16[256,1024]{1,0:T(8,128)(2,1)}, u32[]{:S(2)}) copy-start(bf16[256,1024]{1,0:T(8,128)(2,1)} %refs_1_.7) | copy-start | bytes 1572868

commit v5 on v4

--- a/solution.py
+++ b/solution.py
@@ -249,18 +249,19 @@
         io.send(h)
 
 
-PAIR = 2
-
-
 class Stream:
-    def __init__(self, chunks, arrivals, departures, spare, sem):
-        self.chunks, self.arrivals, self.departures = chunks, arrivals, departures
+    def __init__(self, heads, bring, take, ahead, arrivals, departures, spare, sem):
+        self.heads, self.bring, self.take, self.ahead = heads, bring, take, ahead
+        self.arrivals, self.departures = arrivals, departures
         self.spare, self.sem = spare, sem
         if spare is not None:
             self.early = self.copy(*spare)
-        for i in range(chunks):
-            for copy in arrivals:
-                copy(i).start()
+        for i in range(min(ahead, heads // bring)):
+            self.begin(i)
+
+    def begin(self, i):
+        for copy in self.arrivals:
+            copy(i, self.bring).start()
 
     def copy(self, source, target):
         copy = pltpu.make_async_copy(source, target, self.sem)
@@ -272,33 +273,40 @@
         return self.spare[1]
 
     def need(self, h):
-        if h % PAIR == 0:
+        i, inside = divmod(h, self.bring)
+        if inside == 0:
             for copy in self.arrivals:
-                copy(h // PAIR).wait()
+                copy(i, self.bring).wait()
+            if (i + self.ahead) * self.bring < self.heads:
+                self.begin(i + self.ahead)
 
     def send(self, h):
-        if h % PAIR == PAIR - 1:
+        i, inside = divmod(h, self.take)
+        if inside == self.take - 1:
             for copy in self.departures:
-                copy(h // PAIR).start()
+                copy(i, self.take).start()
 
     def finish(self):
-        for i in range(self.chunks):
+        for i in range(self.heads // self.take):
             for copy in self.departures:
-                copy(i).wait()
-
-
-def chunk_of(ref, i):
+                copy(i, self.take).wait()
+
+
+def run_of(ref, i, n):
     if len(ref.shape) == 3:
-        return ref.at[pl.ds(i * PAIR, PAIR)]
-    return ref.at[:, pl.ds(i * PAIR * HD, PAIR * HD)]
-
-
-def copier(source, target, sem, n):
-    return lambda i: pltpu.make_async_copy(chunk_of(source, i), chunk_of(target, i), sem.at[n, i])
+        return ref.at[pl.ds(i * n, n)]
+    return ref.at[:, pl.ds(i * n * HD, n * HD)]
+
+
+def copier(source, target, sem, j):
+    return lambda i, n: pltpu.make_async_copy(
+        run_of(source, i, n), run_of(target, i, n), sem.at[j, i]
+    )
 
 
 def call(
-    kernel, outs, *args, stream_in=0, raw=0, fetch=False, stream_out=0, chunks=1, flops=0, limit=16
+    kernel, outs, *args, stream_in=0, raw=0, fetch=False, stream_out=0,
+    heads=8, bring=2, take=2, ahead=8, flops=0, limit=16,
 ):
     moved = sum(a.size * a.dtype.itemsize for a in args)
     moved += sum(s.size * s.dtype.itemsize for s in outs)
@@ -317,7 +325,9 @@
             departures.append(copier(local, results[j], scratch[-1], j))
             results[j] = local
         spare = (ins[stream_in], scratch[stream_in + stream_out]) if fetch else None
-        io = Stream(chunks, arrivals, departures, spare, scratch[-3].at[0])
+        io = Stream(
+            heads, bring, take, ahead, arrivals, departures, spare, scratch[-3].at[0]
+        )
         kernel(io, *ins, *results)
         io.finish()
 
@@ -337,8 +347,8 @@
         scratch_shapes=[pltpu.VMEM(s.shape, s.dtype) for s in streamed]
         + [
             pltpu.SemaphoreType.DMA((1,)),
-            pltpu.SemaphoreType.DMA((max(stream_in, 1), chunks)),
-            pltpu.SemaphoreType.DMA((max(stream_out, 1), chunks)),
+            pltpu.SemaphoreType.DMA((max(stream_in, 1), heads // bring)),
+            pltpu.SemaphoreType.DMA((max(stream_out, 1), heads // take)),
         ],
         compiler_params=pltpu.CompilerParams(vmem_limit_bytes=limit * MIB),
         cost_estimate=pl.CostEstimate(flops=flops, bytes_accessed=moved, transcendentals=0),
@@ -363,7 +373,6 @@
     gain = out_gain[None, :]
     decay = log_decay.T
     product = 2 * tokens * HD * HD * heads
-    chunks = heads // PAIR
 
     def exchange(value, axis, members=None):
         return lax.all_to_all(value, axis, 0, 0, axis_index_groups=members)
@@ -372,7 +381,7 @@
         state_kernel,
         [shape((heads, HD + 8, HD)), shape((tokens, heads))],
         key_rows, value_rows, decay,
-        stream_in=2, raw=1, fetch=True, stream_out=1, chunks=chunks, flops=product,
+        stream_in=2, raw=1, fetch=True, stream_out=1, heads=heads, bring=heads, take=4, flops=product,
     )
     parts = exchange(parts, "seq", near)
     within, norm_grad, mixing, scaled, grown, prior = call(
@@ -382,7 +391,7 @@
             shape((heads, HD, tokens), BF16), shape((tokens, heads)), shape((1, HD, HD)),
         ],
         queries, key_rows, value_rows, gate_input, out_grad, prior_state, decay, gain,
-        stream_in=5, raw=1, stream_out=4, chunks=chunks, flops=4 * product, limit=24,
+        stream_in=5, raw=1, stream_out=4, heads=heads, ahead=2, flops=4 * product, limit=24,
     )
     total, factor = call(
         forward_total_kernel,
@@ -406,7 +415,7 @@
         gradient_kernel,
         [shape(states), shape((tokens, HD)), shape((tokens, HD))],
         scaled, norm_grad, sums, context,
-        stream_out=1, chunks=chunks, flops=product,
+        stream_out=1, heads=heads, take=4, flops=product,
     )
     parts = exchange(parts, "seq", near)
     attended, grad_gate, grad_query, part_k, part_v = call(
@@ -414,7 +423,7 @@
         [shape(wide, BF16), shape(wide, BF16), shape(wide, BF16), shape(wide), shape(wide)],
         queries, key_rows, value_rows, gate_input, norm_grad, context, mixing, opening,
         decay, grown, gain, inverse, slope,
-        stream_in=8, stream_out=5, chunks=chunks, flops=9 * product, limit=32,
+        stream_in=8, stream_out=5, heads=heads, ahead=2, flops=9 * product, limit=32,
     )
     (total,) = call(
         backward_total_kernel,
@@ -430,7 +439,7 @@
         finish_kernel,
         [shape(wide, BF16), shape(wide, BF16)],
         key_rows, value_rows, part_k, part_v, returned, remain,
-        stream_out=2, chunks=chunks, flops=2 * product,
+        stream_out=2, heads=heads, flops=2 * product,
     )
     return attended, grad_query, grad_key, grad_value, grad_gate
 

time: 104 us -> 103 us (level)
  transfers between devices with their start and end apart: 2 -> 2, of which waited for: 2 -> 2; matrix products, arithmetic and copies ran while one was open for 0% -> 0% of each run, Pallas kernels for 10% -> 11%
where the time goes in v5:
time: 103 us
  blocking collectives  66.4 us (64%)
  Pallas kernels  18 us (17%)
  starting transfers between devices  9.17 us (9%)
  waiting for transfers between devices  8.42 us (8%)
    all_to_all x5, blocking collectives, exchange(): return lax.all_to_all(value, axis, 0, 0, axis_index_groups=members)  66.4 us
    pallas_call x10, Pallas kernels, call(): pl.pallas_call(body, out_shape=tuple(shapes), in_specs=[outside] * (strea...  18 us
    all_to_all x2, starting transfers between devices, exchange(): return lax.all_to_all(value, axis, 0, 0, axis_index_groups=members)  9.17 us
    all_to_all x2, waiting for transfers between devices, exchange(): return lax.all_to_all(value, axis, 0, 0, axis_index_groups=members)  8.42 us
  transfers between devices with their start and end apart: 2, of which 2 were waited for; matrix products, arithmetic and copies ran while one was open for 0% of the time, Pallas kernels for 11%

profile of v5, /device:TPU:8, one launch (start us, length us, event | category | flops | bytes accessed | tf_op | source)
XLA Modules:
  0.0 102.8 jit_solution(1469327845224737707)
XLA Ops:
  0.6 2.6 %state_kernel.1 = (f32[8,136,128]{2,1,0:T(8,128)}, f32[256,8]{1,0:T(8,128)S(1)}) custom-call(bf16[256,1024]{1,0:T(8,128)(2,1)} %refs_0_.9, bf16[256,1024]{1,0:T(8,128)(2,1)} %refs_1_.7, f32[8,256]{1,0:T(8,128)} %bitcast.2), custom_call_target="tpu_custom_call" | custom-call | flops 67108864 | bytes 1622016 | tf_op jit(solution)/shard_map/state_kernel/pallas_call | solution.py:342
  3.3 0.0 copy-start.10
  3.3 0.0 copy-start.11
  3.3 5.7 %all-to-all-start = ((f32[8,136,128]{2,1,0:T(8,128)}), f32[8,136,128]{2,1,0:T(8,128)S(1)}, u32[]{:S(2)}, u32[]{:S(2)}) async-start(f32[8,136,128]{2,1,0:T(8,128)} %get-tuple-element.32), calls=%async_computation | async-start | bytes 1114112 | tf_op jit(solution)/shard_map/all_to_all | solution.py:378
  9.0 5.0 %within_kernel.1 = (f32[256,1024]{1,0:T(8,128)}, f32[256,1024]{1,0:T(8,128)}, bf16[8,256,256]{2,1,0:T(8,128)(2,1)}, bf16[8,128,256]{2,1,0:T(8,128)(2,1)}, f32[25...) custom-call(bf16[256,1024]{1,0:T(8,128)(2,1)} %refs_0_.8, bf16[256,1024]{1,0:T(8,128)(2,1)} %refs_0_.9, ...), custom_call_target="tpu_custom_call" | custom-call | flops 268435456 | bytes 6901760 | tf_op jit(solution)/shard_map/within_kernel/pallas_call | solution.py:342
  14.0 4.7 %all-to-all-done.refs_1_.refs_0_ = f32[8,136,128]{2,1,0:T(8,128)S(1)} async-done(((f32[8,136,128]{2,1,0:T(8,128)}), f32[8,136,128]{2,1,0:T(8,128)S(1)}, u32[]{:S(2)}, u32[]{:S(2)}) %all-to-all-start) | async-done | bytes 557088 | tf_op jit(solution)/shard_map/all_to_all | solution.py:378
  18.7 0.1 forward_total_kernel.1
  18.9 18.0 %all_to_all.35.refs_1_ = f32[4,136,128]{2,1,0:T(8,128)S(1)} all-to-all(f32[4,136,128]{2,1,0:T(8,128)S(1)} %get-tuple-element.33), channel_id=1, replica_groups={{0,64,128,192},{8,72,136,200},{16,80,144,208},{24,88,152,216},{32,96,16..., dimensions={0} | all-to-all | bytes 557056 | tf_op jit(solution)/shard_map/all_to_all | solution.py:378
  36.9 0.1 forward_chain_kernel.1
  37.0 12.9 %all_to_all.36.refs_4_.refs_7_ = f32[8,128,128]{2,1,0:T(8,128)S(1)} all-to-all(f32[8,128,128]{2,1,0:T(8,128)S(1)} %get-tuple-element.36), channel_id=1, replica_groups={{0,8,16,24,32,40,48,56},{64,72,80,88,96,104,112,120},{128,136,144,152,1..., dimensions={0} | all-to-all | bytes 1048576 | tf_op jit(solution)/shard_map/all_to_all | solution.py:378
  50.0 0.0 copy-start.9
  50.0 0.9 context_kernel.1
  50.9 8.6 %all_to_all.37.refs_2_ = f32[8,2,256]{2,1,0:T(2,128)S(1)} all-to-all(f32[8,2,256]{2,1,0:T(2,128)S(1)} %get-tuple-element.40), channel_id=1, replica_groups=mesh['seq'=32,'head'=8] {'head'}, dimensions={0} | all-to-all | bytes 32768 | tf_op jit(solution)/shard_map/all_to_all | solution.py:378
  59.6 1.6 %gradient_kernel.1 = (f32[8,128,128]{2,1,0:T(8,128)}, f32[256,128]{1,0:T(8,128)S(1)}, f32[256,128]{1,0:T(8,128)S(1)}) custom-call(bf16[8,128,256]{2,1,0:T(8,128)(2,1)S(1)} %copy-done.9, f32[256,1024]{1,0:T(8,128)S(1)} %copy-done, f32[8,2,256]{2,1,0:T(2,128)S(1)} %all_to_all.37.refs_2_, f32[256,1024]{1,0:T(8,128)S(1)} %get-tuple-element.37.refs_3_.refs_5_), custom_call_target="tpu_custom_call" | custom-call | flops 67108864 | bytes 3424256 | tf_op jit(solution)/shard_map/gradient_kernel/pallas_call | solution.py:342
  61.2 3.5 %all-to-all-start.4 = ((f32[8,128,128]{2,1,0:T(8,128)}), f32[8,128,128]{2,1,0:T(8,128)S(1)}, u32[]{:S(2)}, u32[]{:S(2)}) async-start(f32[8,128,128]{2,1,0:T(8,128)} %get-tuple-element.47), calls=%async_computation.4 | async-start | bytes 1048576 | tf_op jit(solution)/shard_map/all_to_all | solution.py:378
  64.7 5.9 %local_backward_kernel.1 = (bf16[256,1024]{1,0:T(8,128)(2,1)}, bf16[256,1024]{1,0:T(8,128)(2,1)}, bf16[256,1024]{1,0:T(8,128)(2,1)}, f32[256,1024]{1,0:T(8,128)}, f32[256,1024]{1,0:T(8,128)}) custom-call(bf16[256,1024]{1,0:T(8,128)(2,1)} %refs_0_.8, bf16[256,1024]{1,0:T(8,128)(2,1)} %refs_0_.9, bf16[256,1024]{1,0:T(8,128)(2,1)} %refs_1_.7, ...), custom_call_target="tpu_custom_call" | custom-call | flops 603979776 | bytes 9719808 | tf_op jit(solution)/shard_map/local_backward_kernel/pallas_call | solution.py:342
  70.6 3.7 %all-to-all-done.4.refs_1_.refs_0_ = f32[8,128,128]{2,1,0:T(8,128)S(1)} async-done(((f32[8,128,128]{2,1,0:T(8,128)}), f32[8,128,128]{2,1,0:T(8,128)S(1)}, u32[]{:S(2)}, u32[]{:S(2)}) %all-to-all-start.4) | async-done | bytes 524320 | tf_op jit(solution)/shard_map/all_to_all | solution.py:378
  74.3 0.1 backward_total_kernel.1
  74.4 14.2 %all_to_all.38.refs_1_ = f32[4,128,128]{2,1,0:T(8,128)S(1)} all-to-all(f32[4,128,128]{2,1,0:T(8,128)S(1)} %backward_total_kernel.1), channel_id=1, replica_groups={{0,64,128,192},{8,72,136,200},{16,80,144,208},{24,88,152,216},{32,96,16..., dimensions={0} | all-to-all | bytes 524288 | tf_op jit(solution)/shard_map/all_to_all | solution.py:378
  88.7 0.1 backward_chain_kernel.1
  88.8 0.0 copy-start.1
  88.8 0.0 copy-start.2
  88.8 12.6 %all_to_all.39.refs_4_ = f32[8,128,128]{2,1,0:T(8,128)S(1)} all-to-all(f32[8,128,128]{2,1,0:T(8,128)S(1)} %backward_chain_kernel.1), channel_id=1, replica_groups={{0,8,16,24,32,40,48,56},{64,72,80,88,96,104,112,120},{128,136,144,152,1..., dimensions={0} | all-to-all | bytes 1048576 | tf_op jit(solution)/shard_map/all_to_all | solution.py:378
  101.4 1.4 %finish_kernel.1 = (bf16[256,1024]{1,0:T(8,128)(2,1)}, bf16[256,1024]{1,0:T(8,128)(2,1)}) custom-call(bf16[256,1024]{1,0:T(8,128)(2,1)S(1)} %copy-done.1, bf16[256,1024]{1,0:T(8,128)(2,1)S(1)} %copy-done.2, f32[256,1024]{1,0:T(8,128)S(1)} %copy-done.6, f32[256,1024]{1,0:T(8,128)S(1)} %copy-done.8, f32[8,128,128]{2,1,0:T(8,128)S(1)} %all_to_all.39.refs_4_, ...), custom_call_target="tpu_custom_call" | custom-call | flops 134217728 | bytes 4726784 | tf_op jit(solution)/shard_map/finish_kernel/pallas_call | solution.py:342
  (19 shorter events, 0.0 us)
Async XLA Ops:
  3.3 5.7 %copy-start.10 = (f32[256,8]{0,1:T(8,128)S(1)}, f32[256,8]{0,1:T(8,128)}, u32[]{:S(2)}) copy-start(f32[256,8]{0,1:T(8,128)} %param.11) | copy-start | bytes 24580
  3.3 5.7 %copy-start.11 = (f32[1024]{0:T(1024)S(1)}, f32[1024]{0:T(1024)}, u32[]{:S(2)}) copy-start(f32[1024]{0:T(1024)} %param.13) | copy-start | bytes 12292
  3.3 15.4 %all-to-all-start = ((f32[8,136,128]{2,1,0:T(8,128)}), f32[8,136,128]{2,1,0:T(8,128)S(1)}, u32[]{:S(2)}, u32[]{:S(2)}) async-start(f32[8,136,128]{2,1,0:T(8,128)} %get-tuple-element.32), calls=%async_computation | async-start | bytes 1114112 | tf_op jit(solution)/shard_map/all_to_all | solution.py:378
  18.7 31.3 %copy-start.5 = (f32[256,1024]{1,0:T(8,128)S(1)}, f32[256,1024]{1,0:T(8,128)}, u32[]{:S(2)}) copy-start(f32[256,1024]{1,0:T(8,128)} %get-tuple-element.30.refs_0_.refs_1_) | copy-start | bytes 3145732
  36.9 13.1 %copy-start = (f32[256,1024]{1,0:T(8,128)S(1)}, f32[256,1024]{1,0:T(8,128)}, u32[]{:S(2)}) copy-start(f32[256,1024]{1,0:T(8,128)} %get-tuple-element.29.refs_2_.refs_1_.refs_4_) | copy-start | bytes 3145732
  37.0 12.9 %copy-start.4 = (bf16[256,1024]{1,0:T(8,128)(2,1)S(1)}, bf16[256,1024]{1,0:T(8,128)(2,1)}, u32[]{:S(2)}) copy-start(bf16[256,1024]{1,0:T(8,128)(2,1)} %refs_0_.8) | copy-start | bytes 1572868
  50.0 0.9 copy-start.3
  50.0 9.6 %copy-start.9 = (bf16[8,128,256]{2,1,0:T(8,128)(2,1)S(1)}, bf16[8,128,256]{2,1,0:T(8,128)(2,1)}, u32[]{:S(2)}) copy-start(bf16[8,128,256]{2,1,0:T(8,128)(2,1)} %get-tuple-element.39.refs_0_) | copy-start | bytes 1572868
  50.9 10.2 %copy-start.7 = (f32[256,1024]{1,0:T(8,128)}, f32[256,1024]{1,0:T(8,128)S(1)}, u32[]{:S(2)}) copy-start(f32[256,1024]{1,0:T(8,128)S(1)} %get-tuple-element.37.refs_3_.refs_5_) | copy-start | bytes 3145732
  61.2 13.1 %all-to-all-start.4 = ((f32[8,128,128]{2,1,0:T(8,128)}), f32[8,128,128]{2,1,0:T(8,128)S(1)}, u32[]{:S(2)}, u32[]{:S(2)}) async-start(f32[8,128,128]{2,1,0:T(8,128)} %get-tuple-element.47), calls=%async_computation.4 | async-start | bytes 1048576 | tf_op jit(solution)/shard_map/all_to_all | solution.py:378
  74.3 27.1 %copy-start.8 = (f32[256,1024]{1,0:T(8,128)S(1)}, f32[256,1024]{1,0:T(8,128)}, u32[]{:S(2)}) copy-start(f32[256,1024]{1,0:T(8,128)} %get-tuple-element.46.refs_3_) | copy-start | bytes 3145732
  88.7 12.8 %copy-start.6 = (f32[256,1024]{1,0:T(8,128)S(1)}, f32[256,1024]{1,0:T(8,128)}, u32[]{:S(2)}) copy-start(f32[256,1024]{1,0:T(8,128)} %get-tuple-element.45.refs_0_.refs_2_) | copy-start | bytes 3145732
  88.8 12.6 %copy-start.1 = (bf16[256,1024]{1,0:T(8,128)(2,1)S(1)}, bf16[256,1024]{1,0:T(8,128)(2,1)}, u32[]{:S(2)}) copy-start(bf16[256,1024]{1,0:T(8,128)(2,1)} %refs_0_.9) | copy-start | bytes 1572868
  88.8 12.6 %copy-start.2 = (bf16[256,1024]{1,0:T(8,128)(2,1)S(1)}, bf16[256,1024]{1,0:T(8,128)(2,1)}, u32[]{:S(2)}) copy-start(bf16[256,1024]{1,0:T(8,128)(2,1)} %refs_1_.7) | copy-start | bytes 1572868
